TPU v7x, 128 devices: a whole 4x4x4 slice. The times are simulated.
128 devices in a mesh: tm: 16 (over y, z), env: 8 (over x, core).
Axes of the slice: x: 4, y: 4, z: 4, core: 2. Of those that a mesh axis runs over, the one named last changes fastest.
Arguments:
- rewards: float32 [32768, 4096], P('tm', 'env'), may hold values from -0.16 to 0.16
- values: float32 [32768, 4096], P('tm', 'env'), may hold values from -6 to 6
- last_value: float32 [4096], P('env'), may hold values from -6 to 6
- done_steps: int32 [4096, 4], P('env'), may hold values from 0 to 32767
- horizon_offset: int32 [4096], P('env'), may hold values from 0 to 16383
- discount_rate: float32 [4096], P('env'), may hold values from 1.5258789e-06 to 0.03
- trace_rate: float32 [4096], P('env'), may hold values from 1.5258789e-06 to 0.03
Outputs:
- norm_advantages: float32 [4096, 32768], P(('env', 'tm'))
- norm_returns: float32 [4096, 32768], P(('env', 'tm'))
Inputs may be any that keep to these rules, and one draw needn't show every extreme that they name: `done_steps`: a repeated step in one environment's list is one termination.
All inputs are finite; a program needn't handle non-finite values.
Results may differ from a plain program's by a relative error of at most 0.0008.
Values sent between devices are 32-bit elements; how exact they have to be, the bound alone decides.
No kernel may reach another device: no remote copies, remote signals or barrier semaphores. Data moves between devices by JAX's collectives and lax.ppermute only.
A program may use at most 128 MiB of HBM per device.

v0:
```python
import jax
import jax.numpy as jnp
from jax import lax
from jax.sharding import Mesh
from jax.sharding import PartitionSpec as P

TM = ("tm_0", "tm_1")
ENV = ("env_0", "env_1")
TM_ENV = ("tm_0", "tm_1", "env_0", "env_1")
ENV_TM = ("env_0", "env_1", "tm_0", "tm_1")


def by_axis(value, axes):
    for axis in axes:
        value = lax.psum(value, axis)
    return value


def from_behind(block, axis, distance):
    devices = range(lax.axis_size(axis))
    route = [(i - distance, i) for i in devices if i - distance in devices]
    return lax.ppermute(block, axis, route)


def copy_for_each(value, axis):
    size = lax.axis_size(axis)
    return lax.all_to_all(
        jnp.broadcast_to(value[None], (size, *value.shape)), axis, 0, 0, tiled=True
    )


def all_in_one(value, axis):
    leaves = jax.tree.leaves(value)
    order = sorted(range(len(leaves)), key=lambda k: -leaves[k].size)
    width = (1, *leaves[order[0]].shape)[-1]
    lines = [
        jnp.pad(leaves[k].reshape(-1), (0, -leaves[k].size % width)).reshape(-1, width)
        for k in order
    ]
    both, at, found = (copy_for_each(jnp.concatenate(lines), axis), 0, {})
    for k, line in zip(order, lines):
        piece = both[:, at : at + len(line)].reshape(len(both), -1)
        found[k] = piece[:, : leaves[k].size].reshape(-1, *leaves[k].shape)
        at += len(line)
    numbers = iter(range(len(leaves)))
    return jax.tree.map(lambda _: found[next(numbers)], value)


def combined_pairwise(pieces, combine):
    while len(jax.tree.leaves(pieces)[0]) > 1:
        pieces = jax.vmap(combine)(
            *(jax.tree.map(lambda part: part[side::2], pieces) for side in (0, 1))
        )
    return jax.tree.map(lambda part: part[0], pieces)


def prefix(value, axis, combine, identity):
    size, here = (lax.axis_size(axis), lax.axis_index(axis))
    passed = jnp.arange(size) > here

    def kept(part, zero, own):
        part = jnp.where(
            passed.reshape(-1, *(1 for _ in own.shape)), part, jnp.asarray(zero, own.dtype)
        )
        return part[::-1]

    pieces = all_in_one(value, axis)
    return combined_pairwise(jax.tree.map(kept, pieces, identity, value), combine)


def episode_masks(moment_index, ends, offsets, horizon):
    finished = jnp.zeros_like(moment_index + offsets, dtype=bool)
    for column in ends:
        finished = finished | (moment_index == column)
    truncated = (moment_index + offsets) % horizon == horizon - 1
    living = 1.0 - finished.astype(jnp.float32)
    carried = living * (1.0 - truncated.astype(jnp.float32))
    return (living, carried)


def shift_later(field, distance, axis, filler):
    length = field.shape[axis]
    kept = lax.slice_in_dim(field, distance, length, 1, axis)
    shape = list(field.shape)
    shape[axis] = distance
    pad_block = jnp.full(tuple(shape), filler, field.dtype)
    return jnp.concatenate([kept, pad_block], axis=axis)


def suffix_scan(td_error, decay, axis):
    length = td_error.shape[axis]
    partial_value = td_error
    decayed = decay
    distance = 1
    while distance < length:
        later_partial = shift_later(partial_value, distance, axis, 0.0)
        later_decayed = shift_later(decayed, distance, axis, 1.0)
        partial_value = partial_value + decayed * later_partial
        decayed = decayed * later_decayed
        distance = distance * 2
    return (partial_value, decayed)


def compose_blocks(earlier, later):
    return (later[0] + later[1] * earlier[0], later[1] * earlier[1])


def statistics(advantages, returns):
    devices = lax.axis_size(TM) * lax.axis_size(ENV)
    samples = float(advantages.size * devices)
    sum_adv, sum_ret = (by_axis(jnp.sum(advantages), TM_ENV), by_axis(jnp.sum(returns), TM_ENV))
    mean_adv = sum_adv / samples
    mean_ret = sum_ret / samples
    dev_adv = advantages - mean_adv
    dev_ret = returns - mean_ret
    sq_adv, sq_ret = (
        by_axis(jnp.sum(dev_adv * dev_adv), TM_ENV),
        by_axis(jnp.sum(dev_ret * dev_ret), TM_ENV),
    )
    var_adv = sq_adv / samples
    var_ret = sq_ret / samples
    norm_adv = (advantages - mean_adv) / jnp.sqrt(var_adv + 1e-05)
    norm_ret = (returns - mean_ret) / jnp.sqrt(var_ret + 1e-05)
    return (norm_adv, norm_ret)


def shards(rewards, values, last_value, done_steps, horizon_offset, discount_rate, trace_rate):
    steps_dev, envs_dev = rewards.shape
    time_blocks = lax.axis_size(TM)
    position = lax.axis_index(TM)
    horizon = steps_dev * time_blocks // 2
    discount = jnp.exp(-discount_rate)
    retention = discount * jnp.exp(-trace_rate)
    moment_index = position * steps_dev + jnp.arange(steps_dev, dtype=jnp.int32)[:, None]
    ends = [done_steps[:, column][None, :] for column in range(done_steps.shape[1])]
    living, carried = episode_masks(moment_index, ends, horizon_offset[None, :], horizon)
    first_next = from_behind(values[0:1], TM, -1)
    boundary = jnp.where(position == time_blocks - 1, last_value[None, :], first_next)
    next_value = jnp.concatenate([values[1:], boundary], axis=0)
    td_error = rewards + discount[None, :] * living * next_value - values
    decay = retention[None, :] * carried
    partial_value, decayed = suffix_scan(td_error, decay, 0)
    identity = (jnp.zeros_like(partial_value[0]), jnp.ones_like(decayed[0]))
    incoming = prefix((partial_value[0], decayed[0]), TM, compose_blocks, identity)[0]
    advantages = partial_value + decayed * incoming[None, :]
    returns = advantages + values
    norm_adv, norm_ret = statistics(advantages, returns)
    return (
        lax.all_to_all(norm_adv.T, TM, split_axis=0, concat_axis=1, tiled=True),
        lax.all_to_all(norm_ret.T, TM, split_axis=0, concat_axis=1, tiled=True),
    )


def solution(mesh):
    split = Mesh(mesh.devices.reshape(4, 4, 4, 2), ("tm_0", "tm_1", "env_0", "env_1"))
    placed = (P(TM, ENV), P(TM, ENV), P(ENV), P(ENV, None), P(ENV), P(ENV), P(ENV))
    return jax.shard_map(
        shards,
        mesh=split,
        in_specs=placed,
        out_specs=(P(ENV_TM, None), P(ENV_TM, None)),
        check_vma=False,
    )
```

profile of v0, /device:TPU:114, one launch (start us, length us, event | category | flops | bytes accessed | tf_op | source)
XLA Modules:
  0.0 445.8 jit_solution(117539721496437873)
XLA Ops:
  21.4 6.0 %fusion.3 = f32[2048,512]{0,1:T(8,128)S(1)} fusion(f32[2048,512]{0,1:T(8,128)} %copy.25, f32[2048,512]{0,1:T(8,128)} %copy.27, f32[1,512]{0,1:T(8,128)S(1)} %copy.26, f32[2047,512]{0,1:T(8,128)} %slice.207, f32[512]{0:T(512)S(1)} %get-tuple-element.54, s32[512]{0:T(512)S(1)} %bitcast.34, s32[512]{0:T(512)S(1)} %bitcast.37, s32[512]{0:T(512)S(1)} %bitcast.31, ...), kind=kLoop, calls=%fused_computation.9 | loop fusion | flops 14680064 | bytes 16795648 | tf_op jit(solution)/shard_map/sub | solution.py:140
  36.1 6.0 %multiply_add_fusion.10 = (f32[2048,512]{0,1:T(8,128)S(1)}, f32[2048,512]{0,1:T(8,128)S(1)}) fusion(f32[2048,512]{0,1:T(8,128)S(1)} %get-tuple-element.44, f32[2046,512]{0,1:T(8,128)S(1)} %slice.210, f32[2047,512]{0,1:T(8,128)S(1)} %slice.209, s32[512]{0:T(512)S(1)} %copy-done.18, s32[512]{0:T(512)S(1)} %bitcast.36, s32[512]{0:T(512)S(1)} %bitcast.39, ...), kind=kLoop, calls=%fused_computation.32 | loop fusion | flops 30408704 | bytes 20985856 | tf_op jit(solution)/shard_map/add | solution.py:98
  48.6 10.2 %multiply_add_fusion.9 = (f32[2048,512]{0,1:T(8,128)}, f32[2048,512]{0,1:T(8,128)}) fusion(f32[2048,512]{0,1:T(8,128)S(1)} %get-tuple-element.39, f32[2044,512]{0,1:T(8,128)} %slice.212, f32[2048,512]{0,1:T(8,128)} %copy-done, f32[2046,512]{0,1:T(8,128)} %slice.211), kind=kLoop, calls=%fused_computation.30 | loop fusion | flops 3145728 | bytes 25153536 | tf_op jit(solution)/shard_map/add | solution.py:98
  58.8 5.5 %slice.214 = f32[2040,512]{0,1:T(8,128)} slice(f32[2048,512]{0,1:T(8,128)} %get-tuple-element.37), slice={[8:2048], [0:512]} | slice | bytes 8355840 | tf_op jit(solution)/shard_map/slice | solution.py:83
  67.4 10.2 %multiply_add_fusion.8 = (f32[2048,512]{0,1:T(8,128)}, f32[2048,512]{0,1:T(8,128)}) fusion(f32[2048,512]{0,1:T(8,128)S(1)} %copy-done.1, f32[2040,512]{0,1:T(8,128)} %slice.214, f32[2048,512]{0,1:T(8,128)} %get-tuple-element.38, f32[2044,512]{0,1:T(8,128)} %slice.213), kind=kLoop, calls=%fused_computation.28 | loop fusion | flops 3145728 | bytes 25141248 | tf_op jit(solution)/shard_map/add | solution.py:98
  86.2 10.3 %multiply_add_fusion.7 = (f32[2048,512]{0,1:T(8,128)}, f32[2048,512]{0,1:T(8,128)}) fusion(f32[2048,512]{0,1:T(8,128)S(1)} %copy-done.3, f32[2032,512]{0,1:T(8,128)} %slice.216, f32[2048,512]{0,1:T(8,128)} %get-tuple-element.36, f32[2040,512]{0,1:T(8,128)} %slice.215), kind=kLoop, calls=%fused_computation.26 | loop fusion | flops 3145728 | bytes 25116672 | tf_op jit(solution)/shard_map/add | solution.py:98
  105.1 10.2 %multiply_add_fusion.6 = (f32[2048,512]{0,1:T(8,128)}, f32[2048,512]{0,1:T(8,128)}) fusion(f32[2048,512]{0,1:T(8,128)S(1)} %copy-done.5, f32[2016,512]{0,1:T(8,128)} %slice.218, f32[2048,512]{0,1:T(8,128)} %get-tuple-element.34, f32[2032,512]{0,1:T(8,128)} %slice.217), kind=kLoop, calls=%fused_computation.24 | loop fusion | flops 3145728 | bytes 25067520 | tf_op jit(solution)/shard_map/add | solution.py:98
  123.9 10.2 %multiply_add_fusion.5 = (f32[2048,512]{0,1:T(8,128)}, f32[2048,512]{0,1:T(8,128)}) fusion(f32[2048,512]{0,1:T(8,128)S(1)} %copy-done.7, f32[1984,512]{0,1:T(8,128)} %slice.220, f32[2048,512]{0,1:T(8,128)} %get-tuple-element.32, f32[2016,512]{0,1:T(8,128)} %slice.219), kind=kLoop, calls=%fused_computation.22 | loop fusion | flops 3145728 | bytes 24969216 | tf_op jit(solution)/shard_map/add | solution.py:98
  141.6 10.0 %multiply_add_fusion.4 = (f32[2048,512]{0,1:T(8,128)}, f32[2048,512]{0,1:T(8,128)}) fusion(f32[2048,512]{0,1:T(8,128)} %get-tuple-element.29, f32[1920,512]{0,1:T(8,128)} %slice.222, f32[2048,512]{0,1:T(8,128)S(1)} %copy-done.9, f32[1984,512]{0,1:T(8,128)} %slice.221), kind=kLoop, calls=%fused_computation.20 | loop fusion | flops 3145728 | bytes 24772608 | tf_op jit(solution)/shard_map/add | solution.py:98
  156.2 8.3 %multiply_add_fusion.3 = (f32[2048,512]{0,1:T(8,128)}, f32[2048,512]{0,1:T(8,128)}) fusion(f32[2048,512]{0,1:T(8,128)} %get-tuple-element.27, f32[1792,512]{0,1:T(8,128)} %slice.224, f32[2048,512]{0,1:T(8,128)S(1)} %copy-done.10, f32[1920,512]{0,1:T(8,128)S(1)} %slice.223), kind=kLoop, calls=%fused_computation.18 | loop fusion | flops 3145728 | bytes 24379392 | tf_op jit(solution)/shard_map/add | solution.py:98
  172.0 8.0 %multiply_add_fusion.2 = (f32[2048,512]{0,1:T(8,128)}, f32[2048,512]{0,1:T(8,128)}) fusion(f32[2048,512]{0,1:T(8,128)S(1)} %copy-done.12, f32[1536,512]{0,1:T(8,128)} %slice.226, f32[2048,512]{0,1:T(8,128)S(1)} %copy-done.11, f32[1792,512]{0,1:T(8,128)} %slice.225), kind=kLoop, calls=%fused_computation.16 | loop fusion | flops 3145728 | bytes 23592960 | tf_op jit(solution)/shard_map/add | solution.py:98
  186.6 6.7 %multiply_add_fusion.1 = (f32[2048,512]{0,1:T(8,128)S(1)}, f32[2048,512]{0,1:T(8,128)}) fusion(f32[2048,512]{0,1:T(8,128)S(1)} %copy-done.14, f32[1024,512]{0,1:T(8,128)} %slice.228, f32[2048,512]{0,1:T(8,128)S(1)} %copy-done.13, f32[1536,512]{0,1:T(8,128)} %slice.227), kind=kLoop, calls=%fused_computation.14 | loop fusion | flops 3145728 | bytes 22020096 | tf_op jit(solution)/shard_map/add | solution.py:98
  202.0 7.1 %all-to-all-start = ((f32[16,2,512]{2,1,0:T(2,128)}), f32[16,2,512]{2,1,0:T(2,128)S(1)}, u32[]{:S(2)}, u32[]{:S(2)}) async-start(f32[16,2,512]{2,1,0:T(2,128)} %broadcast_in_dim.20), calls=%async_computation | async-start | bytes 131072 | tf_op jit(solution)/shard_map/all_to_all | solution.py:27
  213.9 11.1 %fusion.6 = (f32[]{:T(128)}, f32[2048,512]{0,1:T(8,128)}, f32[2048,512]{0,1:T(8,128)}) fusion(f32[2048,512]{0,1:T(8,128)} %copy.25, f32[2048,512]{0,1:T(8,128)} %copy-done.17, f32[2048,512]{0,1:T(8,128)} %copy-done.16, f32[512]{0:T(512)S(1)} %bitcast.40), kind=kLoop, calls=%fused_computation.55 | loop fusion | flops 4194303 | bytes 20973572 | tf_op jit(solution)/shard_map/reduce_sum | solution.py:111
  228.8 9.1 %all-reduce.27 = (f32[]{:T(128)}, f32[]{:T(128)}) all-reduce(f32[]{:T(128)} %reduce_sum.36, f32[]{:T(128)} %get-tuple-element.18), channel_id=1, replica_groups=mesh['tm_0'=4,'tm_1'=4,'env_0'=4,'env_1'=2] {'tm_0'}, use_global_device_ids=true, to_apply=%region_1.2 | all-reduce | flops 2 | bytes 16 | tf_op jit(solution)/shard_map/psum | solution.py:15
  238.0 9.2 %all-reduce.25 = (f32[]{:T(128)}, f32[]{:T(128)}) all-reduce(f32[]{:T(128)} %get-tuple-element.12, f32[]{:T(128)} %get-tuple-element.13), channel_id=1, replica_groups=mesh['tm_0'=4,'tm_1'=4,'env_0'=4,'env_1'=2] {'tm_1'}, use_global_device_ids=true, to_apply=%region_2.3 | all-reduce | flops 2 | bytes 16 | tf_op jit(solution)/shard_map/psum | solution.py:15
  247.2 9.2 %all-reduce.23 = (f32[]{:T(128)}, f32[]{:T(128)}) all-reduce(f32[]{:T(128)} %get-tuple-element.8, f32[]{:T(128)} %get-tuple-element.9), channel_id=1, replica_groups=mesh['tm_0'=4,'tm_1'=4,'env_0'=4,'env_1'=2] {'env_0'}, use_global_device_ids=true, to_apply=%region_3.4 | all-reduce | flops 2 | bytes 16 | tf_op jit(solution)/shard_map/psum | solution.py:15
  266.4 9.3 %all-reduce.26 = (f32[]{:T(128)}, f32[]{:T(128)}) all-reduce(f32[]{:T(128)} %get-tuple-element.58, f32[]{:T(128)} %get-tuple-element.57), channel_id=1, replica_groups=mesh['tm_0'=4,'tm_1'=4,'env_0'=4,'env_1'=2] {'tm_0'}, use_global_device_ids=true, to_apply=%region_6.7 | all-reduce | flops 2 | bytes 16 | tf_op jit(solution)/shard_map/psum | solution.py:15
  275.7 9.6 %all-reduce.24 = (f32[]{:T(128)}, f32[]{:T(128)}) all-reduce(f32[]{:T(128)} %get-tuple-element.10, f32[]{:T(128)} %get-tuple-element.11), channel_id=1, replica_groups=mesh['tm_0'=4,'tm_1'=4,'env_0'=4,'env_1'=2] {'tm_1'}, use_global_device_ids=true, to_apply=%region_7.8 | all-reduce | flops 2 | bytes 16 | tf_op jit(solution)/shard_map/psum | solution.py:15
  285.3 10.8 %all-reduce.22 = (f32[]{:T(128)}, f32[]{:T(128)}) all-reduce(f32[]{:T(128)} %get-tuple-element.6, f32[]{:T(128)} %get-tuple-element.7), channel_id=1, replica_groups=mesh['tm_0'=4,'tm_1'=4,'env_0'=4,'env_1'=2] {'env_0'}, use_global_device_ids=true, to_apply=%region_8.9 | all-reduce | flops 2 | bytes 16 | tf_op jit(solution)/shard_map/psum | solution.py:15
  304.8 8.4 %all-to-all-start.1 = ((f32[16,32,2048]{2,1,0:T(8,128)}), f32[16,32,2048]{2,1,0:T(8,128)}, u32[]{:S(2)}, u32[]{:S(2)}) async-start(f32[16,32,2048]{2,1,0:T(8,128)} %bitcast.24), calls=%async_computation.1 | async-start | bytes 8388608 | tf_op jit(solution)/shard_map/all_to_all | solution.py:149
  318.9 56.0 %all-to-all-done.1 = f32[16,32,2048]{2,1,0:T(8,128)} async-done(((f32[16,32,2048]{2,1,0:T(8,128)}), f32[16,32,2048]{2,1,0:T(8,128)}, u32[]{:S(2)}, u32[]{:S(2)}) %all-to-all-start.1) | async-done | bytes 4194336 | tf_op jit(solution)/shard_map/all_to_all | solution.py:149
  374.9 6.9 %all-to-all-start.2 = ((f32[16,32,2048]{2,1,0:T(8,128)}), f32[16,32,2048]{2,1,0:T(8,128)}, u32[]{:S(2)}, u32[]{:S(2)}) async-start(f32[16,32,2048]{2,1,0:T(8,128)} %bitcast.25), calls=%async_computation.2 | async-start | bytes 8388608 | tf_op jit(solution)/shard_map/all_to_all | solution.py:150
  386.5 54.2 %all-to-all-done.2 = f32[16,32,2048]{2,1,0:T(8,128)} async-done(((f32[16,32,2048]{2,1,0:T(8,128)}), f32[16,32,2048]{2,1,0:T(8,128)}, u32[]{:S(2)}, u32[]{:S(2)}) %all-to-all-start.2) | async-done | bytes 4194336 | tf_op jit(solution)/shard_map/all_to_all | solution.py:150
  (112 shorter events, 139.3 us)
Async XLA Ops:
  1.4 19.9 %collective-permute-start = (f32[1,512]{1,0:T(1,128)S(1)}, f32[1,512]{1,0:T(1,128)S(1)}, u32[]{:S(2)}, u32[]{:S(2)}) collective-permute-start(f32[1,512]{1,0:T(1,128)S(1)} %slice.161), channel_id=1, source_target_pairs={{8,0},{16,8},{24,16},{32,24},{40,32},{48,40},{56,48},{64,56},{72,6... | collective-permute-start | bytes 6152 | tf_op jit(solution)/shard_map/ppermute | solution.py:22
  15.9 5.4 %copy-start.19 = (f32[512]{0:T(512)S(1)}, f32[512]{0:T(512)}, u32[]{:S(2)}) copy-start(f32[512]{0:T(512)} %param.9) | copy-start | bytes 6148
  27.4 1.2 copy-start.18
  42.1 3.4 copy-start
  58.8 5.5 %copy-start.2 = (f32[2048,512]{0,1:T(8,128)S(1)}, f32[2048,512]{0,1:T(8,128)}, u32[]{:S(2)}) copy-start(f32[2048,512]{0,1:T(8,128)} %get-tuple-element.38) | copy-start | bytes 12582916
  64.3 3.1 copy-start.1
  77.6 5.5 %copy-start.4 = (f32[2048,512]{0,1:T(8,128)S(1)}, f32[2048,512]{0,1:T(8,128)}, u32[]{:S(2)}) copy-start(f32[2048,512]{0,1:T(8,128)} %get-tuple-element.36) | copy-start | bytes 12582916
  83.1 3.1 copy-start.3
  96.5 5.5 %copy-start.6 = (f32[2048,512]{0,1:T(8,128)S(1)}, f32[2048,512]{0,1:T(8,128)}, u32[]{:S(2)}) copy-start(f32[2048,512]{0,1:T(8,128)} %get-tuple-element.34) | copy-start | bytes 12582916
  102.0 3.1 copy-start.5
  115.3 5.5 %copy-start.8 = (f32[2048,512]{0,1:T(8,128)S(1)}, f32[2048,512]{0,1:T(8,128)}, u32[]{:S(2)}) copy-start(f32[2048,512]{0,1:T(8,128)} %get-tuple-element.32) | copy-start | bytes 12582916
  120.8 3.1 copy-start.7
  134.1 4.4 copy-start.9
  151.6 4.2 copy-start.10
  164.5 4.0 copy-start.11
  168.5 3.5 copy-start.12
  180.0 3.4 copy-start.13
  183.3 3.3 copy-start.14
  193.4 2.0 copy-start.17
  195.5 2.8 copy-start.15
  199.1 2.0 copy-start.16
  202.0 11.1 %all-to-all-start = ((f32[16,2,512]{2,1,0:T(2,128)}), f32[16,2,512]{2,1,0:T(2,128)S(1)}, u32[]{:S(2)}, u32[]{:S(2)}) async-start(f32[16,2,512]{2,1,0:T(2,128)} %broadcast_in_dim.20), calls=%async_computation | async-start | bytes 131072 | tf_op jit(solution)/shard_map/all_to_all | solution.py:27
  304.8 70.1 %all-to-all-start.1 = ((f32[16,32,2048]{2,1,0:T(8,128)}), f32[16,32,2048]{2,1,0:T(8,128)}, u32[]{:S(2)}, u32[]{:S(2)}) async-start(f32[16,32,2048]{2,1,0:T(8,128)} %bitcast.24), calls=%async_computation.1 | async-start | bytes 8388608 | tf_op jit(solution)/shard_map/all_to_all | solution.py:149
  374.9 65.8 %all-to-all-start.2 = ((f32[16,32,2048]{2,1,0:T(8,128)}), f32[16,32,2048]{2,1,0:T(8,128)}, u32[]{:S(2)}, u32[]{:S(2)}) async-start(f32[16,32,2048]{2,1,0:T(8,128)} %bitcast.25), calls=%async_computation.2 | async-start | bytes 8388608 | tf_op jit(solution)/shard_map/all_to_all | solution.py:150
where the time goes:
time: 454 us; the launch traced here: 446 us
  other arithmetic  133 us (29%)
  waiting for transfers between devices  114 us (25%)
  local copies, waits for them, and re-layouts  106 us (23%)
  blocking collectives  63.8 us (14%)
  starting transfers between devices  24.8 us (5%)
    add x10, other arithmetic, suffix_scan(): partial_value = partial_value + decayed * later_partial  90 us
    slice x22, local copies, waits for them, and re-layouts, shift_later(): kept = lax.slice_in_dim(field, distance, length, 1, axis)  69.8 us
    psum x8, blocking collectives, by_axis(): value = lax.psum(value, axis)  63.8 us
    all_to_all x1, waiting for transfers between devices, shards(): lax.all_to_all(norm_adv.T, TM, split_axis=0, concat_axis=1, tiled=True)  56 us
    all_to_all x1, waiting for transfers between devices, shards(): lax.all_to_all(norm_ret.T, TM, split_axis=0, concat_axis=1, tiled=True)  54.2 us
    unnamed x42, local copies, waits for them, and re-layouts  18.3 us
    reduce_sum x1, other arithmetic, statistics(): jnp.sum(returns)  11.1 us
  transfers between devices with their start and end apart: 4, of which 3 were waited for; matrix products, arithmetic and copies ran while one was open for 6% of the time, Pallas kernels for 0%

commit v1 on v0

v1 whole, which is shorter than its diff:
```python
import functools

import jax
import jax.numpy as jnp
from jax import lax
from jax.experimental import pallas as pl
from jax.experimental.pallas import tpu as pltpu
from jax.sharding import Mesh
from jax.sharding import PartitionSpec as P

TM = ("tm_0", "tm_1")
ENV = ("env_0", "env_1")
ALL = ("tm_0", "tm_1", "env_0", "env_1")
ENV_TM = ("env_0", "env_1", "tm_0", "tm_1")
F32 = jnp.float32
LANES = 128
SEG = 32
ROWS = 256
SMEM = pl.BlockSpec(memory_space=pltpu.SMEM)
ANY = pl.BlockSpec(memory_space=pl.ANY)


def params(**kw):
    return pltpu.CompilerParams(vmem_limit_bytes=56 << 20, **kw)


def cost(flops, moved):
    return pl.CostEstimate(flops=flops, transcendentals=0, bytes_accessed=moved)


def pack_body(dests, riders, *refs):
    x_ref, o_ref = refs[0], refs[-1]
    own = x_ref.shape[1] // dests
    base = pl.program_id(0) * (ROWS // LANES) * own if riders else 0
    for h in range(ROWS // LANES):
        tile = x_ref[h * LANES : (h + 1) * LANES, :].T.reshape(dests, own, LANES)
        if riders:
            o_ref[:, pl.ds(pl.multiple_of(base + h * own, own), own), :] = tile
        else:
            o_ref[:, h * own : (h + 1) * own, :] = tile
    if riders:

        @pl.when(pl.program_id(0) == 0)
        def _():
            lines = refs[1][...]
            o_ref[:, o_ref.shape[1] - riders :, :] = jnp.broadcast_to(
                lines[None], (dests, *lines.shape)
            )


def pack(block, dests, start, count, rider=None):
    envs = block.shape[1]
    own = envs // dests
    riders = 0 if rider is None else rider.shape[0]
    rows = count // LANES * own
    per = ROWS // LANES * own
    in_specs = [pl.BlockSpec((ROWS, envs), lambda i: (start // ROWS + i, 0))]
    if riders:
        in_specs.append(pl.BlockSpec(rider.shape, lambda i: (0, 0)))
        out_spec = pl.BlockSpec((dests, rows + riders, LANES), lambda i: (0, 0, 0))
    else:
        out_spec = pl.BlockSpec((dests, per, LANES), lambda i: (0, i, 0))
    return pl.pallas_call(
        functools.partial(pack_body, dests, riders),
        grid=(count // ROWS,),
        in_specs=in_specs,
        out_specs=out_spec,
        out_shape=jax.ShapeDtypeStruct((dests, rows + riders, LANES), F32),
        compiler_params=params(),
        cost_estimate=cost(0, 8 * count * envs),
        name="pack",
    )(block, *(() if rider is None else (rider,)))


def stepper(rew_ref, val_ref, times_ref, rates_ref, length):
    first = lax.broadcasted_iota(jnp.int32, (SEG, LANES), 0) * length
    marks = [
        jnp.broadcast_to(times_ref[k : k + 1, :], (8, LANES))
        for k in range(times_ref.shape[0])
    ]
    marks = [jnp.concatenate([m] * (SEG // 8), axis=0) for m in marks]
    discount = jnp.broadcast_to(rates_ref[0:1, :], (SEG, LANES))
    retention = jnp.broadcast_to(rates_ref[1:2, :], (SEG, LANES))

    def step(i, next_value):
        rows = pl.ds(i, SEG, stride=length)
        reward, value = rew_ref[rows, :], val_ref[rows, :]
        time = first + i
        ended = marks[0] == time
        for mark in marks[1:-1]:
            ended = ended | (mark == time)
        follow = jnp.where(ended, 0.0, discount)
        decay = jnp.where(ended | (marks[-1] == time), 0.0, retention)
        td_error = reward + follow * next_value - value
        return value, td_error, decay, follow

    return step


def value_after(val_ref, boundary, length):
    firsts = val_ref[pl.ds(0, SEG, stride=length), :]
    return jnp.concatenate([firsts[1:], boundary], axis=0)


def summary_body(length, rew_ref, val_ref, times_ref, rates_ref, seg_ref, all_ref):
    step = stepper(rew_ref, val_ref, times_ref, rates_ref, length)
    zero = jnp.zeros((SEG, LANES), F32)

    following = value_after(val_ref, zero[:1], length)
    value, partial, last_decay, last_follow = step(length - 1, following)

    def body(k, carry):
        partial, product, following = carry
        value, td_error, decay, _ = step(length - 2 - k, following)
        return td_error + decay * partial, decay * product, value

    partial, product, _ = lax.fori_loop(
        0, length - 1, body, (partial, zero + 1.0, value), unroll=7
    )
    coefs = product * last_follow
    product = product * last_decay
    seg_ref[0] = partial
    seg_ref[1] = product
    seg_ref[2] = coefs
    s = SEG - 1
    own, kept, coef = partial[s:], product[s:], coefs[s:]
    for s in range(SEG - 2, -1, -1):
        factor = product[s : s + 1]
        own = partial[s : s + 1] + factor * own
        kept = factor * kept
        coef = factor * coef
    lines = jnp.concatenate([own, kept, coef, val_ref[0:1, :]], axis=0)
    all_ref[pl.ds(4 * pl.program_id(0), 4), :] = lines


def columns(*lead):
    return pl.BlockSpec((*lead, LANES), lambda j: (*(0 for _ in lead), j))


def summary(rewards, values, times, rates):
    steps, envs = rewards.shape
    groups = envs // LANES
    return pl.pallas_call(
        functools.partial(summary_body, steps // SEG),
        grid=(groups,),
        in_specs=[columns(steps), columns(steps), columns(len(times)), columns(2)],
        out_specs=[columns(3, SEG), pl.BlockSpec((4 * groups, LANES), lambda j: (0, 0))],
        out_shape=[
            jax.ShapeDtypeStruct((3, SEG, envs), F32),
            jax.ShapeDtypeStruct((4 * groups, LANES), F32),
        ],
        compiler_params=params(),
        cost_estimate=cost(16 * steps * envs, 8 * steps * envs),
        name="summary",
    )(rewards, values, times, rates)


def advantage_body(
    length, here_ref, rew_ref, val_ref, times_ref, rates_ref, last_ref, seg_ref, every_ref, adv_ref, stat_ref
):
    steps = rew_ref.shape[0]
    group = pl.program_id(0)
    here = here_ref[0]
    step = stepper(rew_ref, val_ref, times_ref, rates_ref, length)

    boundary = last_ref[...]
    incoming = jnp.zeros((1, LANES), F32)
    for s in range(every_ref.shape[0] - 1, 0, -1):
        lines = every_ref[s, pl.ds(4 * group, 4), :]
        later = here < s
        start = (lines[0:1] + lines[2:3] * boundary) + lines[1:2] * incoming
        incoming = jnp.where(later, start, incoming)
        boundary = jnp.where(later, lines[3:4], boundary)

    partial, product = seg_ref[0], seg_ref[1]
    after = [incoming]
    for s in range(SEG - 1, 0, -1):
        own = partial[s : s + 1]
        if s == SEG - 1:
            own = own + seg_ref[2, s : s + 1, :] * boundary
        after.append(own + product[s : s + 1] * after[-1])
    after = jnp.concatenate(after[::-1], axis=0)

    def body(k, carry):
        later, following, sum_adv, sum_val = carry
        i = length - 1 - k
        value, td_error, decay, _ = step(i, following)
        own = td_error + decay * later
        adv_ref[pl.ds(i, SEG, stride=length), :] = own
        return own, value, sum_adv + own, sum_val + value

    zero = jnp.zeros((SEG, LANES), F32)
    start = (after, value_after(val_ref, boundary, length), zero, zero)
    _, _, sum_adv, sum_val = lax.fori_loop(0, length, body, start, unroll=8)
    sums = [jnp.sum(sum_adv), jnp.sum(sum_adv + sum_val)]
    mean_adv, mean_ret = [total / (steps * LANES) for total in sums]

    zero = jnp.zeros((64, LANES), F32)

    def spread(k, carry):
        sq_adv, sq_ret = carry
        rows = pl.ds(pl.multiple_of(k * 64, 64), 64)
        own = adv_ref[rows, :]
        off_adv = own - mean_adv
        off_ret = (own + val_ref[rows, :]) - mean_ret
        return sq_adv + off_adv * off_adv, sq_ret + off_ret * off_ret

    sq_adv, sq_ret = lax.fori_loop(0, steps // 64, spread, (zero, zero), unroll=2)
    sums += [jnp.sum(sq_adv), jnp.sum(sq_ret)]
    lane = lax.broadcasted_iota(jnp.int32, stat_ref.shape, 1)

    @pl.when(group == 0)
    def _():
        stat_ref[...] = jnp.zeros(stat_ref.shape, F32)

    line = stat_ref[...]
    for k, total in enumerate(sums):
        line = jnp.where(lane == 4 * group + k, total, line)
    stat_ref[...] = line


def advantage(here, rewards, values, times, rates, last_value, segments, every):
    steps, envs = rewards.shape
    return pl.pallas_call(
        functools.partial(advantage_body, steps // SEG),
        grid=(envs // LANES,),
        in_specs=[
            SMEM, columns(steps), columns(steps), columns(len(times)), columns(2), columns(1),
            columns(3, SEG), pl.BlockSpec(every.shape, lambda j: (0, 0, 0)),
        ],
        out_specs=[columns(steps), pl.BlockSpec((8, LANES), lambda j: (0, 0))],
        out_shape=[
            jax.ShapeDtypeStruct((steps, envs), F32),
            jax.ShapeDtypeStruct((8, LANES), F32),
        ],
        compiler_params=params(),
        cost_estimate=cost(24 * steps * envs, 12 * steps * envs),
        name="advantage",
    )(here, rewards, values, times, rates, last_value, segments, every)


def normal_body(counts, steps, offset, stat_ref, adv, *refs):
    vals = refs[: len(counts)]
    out_adv, out_ret, abuf, vbuf, oabuf, orbuf, in_sem, out_sem = refs[-8:]
    blocks, rows, _ = abuf.shape
    own = out_adv.shape[0]
    width = rows // own * LANES

    def fetches(s):
        copies = [pltpu.make_async_copy(adv.at[s, pl.ds(0, rows)], abuf.at[s], in_sem.at[0, s])]
        at = 0
        for k, (val, count) in enumerate(zip(vals, counts)):
            copies.append(
                pltpu.make_async_copy(
                    val.at[s, pl.ds(0, count)], vbuf.at[s, pl.ds(at, count)], in_sem.at[k + 1, s]
                )
            )
            at += count
        return copies

    def stores(s):
        place = pl.ds(pl.multiple_of(s * steps + offset, LANES), width)
        return [
            pltpu.make_async_copy(buf.at[s], out.at[:, place], out_sem.at[k, s])
            for k, (buf, out) in enumerate(((oabuf, out_adv), (orbuf, out_ret)))
        ]

    def each(body):
        lax.fori_loop(0, blocks, lambda s, c: (body(s), c)[1], 0)

    def begin(s):
        for copy in fetches(s):
            copy.start()

    def work(s):
        for copy in fetches(s):
            copy.wait()
        for h in range(rows // own):
            part = abuf[s, h * own : (h + 1) * own, :]
            ret = part + vbuf[s, h * own : (h + 1) * own, :]
            lanes = slice(h * LANES, (h + 1) * LANES)
            oabuf[s, :, lanes] = (part - stat_ref[0]) * stat_ref[1]
            orbuf[s, :, lanes] = (ret - stat_ref[2]) * stat_ref[3]
        for copy in stores(s):
            copy.start()

    def finish(s):
        for copy in stores(s):
            copy.wait()

    each(begin)
    each(work)
    each(finish)


def normalized(stats, adv, vals, counts, own, steps, offset, into=None):
    blocks, rows = adv.shape[0], sum(counts)
    shape = jax.ShapeDtypeStruct((own, blocks * steps), F32)
    into = () if into is None else tuple(into)
    at = 2 + len(vals)
    width = rows // own * LANES
    return pl.pallas_call(
        functools.partial(normal_body, counts, steps, offset),
        in_specs=[SMEM] + [ANY] * (1 + len(vals) + len(into)),
        out_specs=[ANY, ANY],
        out_shape=[shape, shape],
        input_output_aliases={at + k: k for k in range(len(into))},
        scratch_shapes=[
            pltpu.VMEM((blocks, rows, LANES), F32),
            pltpu.VMEM((blocks, rows, LANES), F32),
            pltpu.VMEM((blocks, own, width), F32),
            pltpu.VMEM((blocks, own, width), F32),
            pltpu.SemaphoreType.DMA((1 + len(vals), blocks)),
            pltpu.SemaphoreType.DMA((2, blocks)),
        ],
        compiler_params=params(),
        cost_estimate=cost(4 * blocks * rows * LANES, 16 * blocks * rows * LANES),
        name="normalized",
    )(stats, adv, *vals, *into)


def exchange(packed, behind=None):
    if behind is not None:
        packed, behind = lax.optimization_barrier((packed, behind))
    return lax.all_to_all(packed, TM, 0, 0, tiled=True), behind


def merged(mean, square, count, axis, distance):
    size = lax.axis_size(axis)
    other = lax.ppermute(
        jnp.concatenate([mean, square]), axis, [(i, (i + distance) % size) for i in range(size)]
    )
    gap = other[:2] - mean
    return mean + 0.5 * gap, square + other[2:] + (0.5 * count) * gap * gap, 2.0 * count


def shards(rewards, values, last_value, done_steps, horizon_offset, discount_rate, trace_rate):
    steps, envs = rewards.shape
    blocks = lax.axis_size(TM)
    here = lax.axis_index(TM)
    horizon = steps * blocks // 2
    groups = envs // LANES
    own = envs // blocks
    half, quarter = steps // 2, steps // 4
    rows = lambda count: count // LANES * own

    val_1, _ = exchange(pack(values, blocks, 0, quarter))

    discount = jnp.exp(-discount_rate)
    rates = jnp.stack([discount, discount * jnp.exp(-trace_rate)])
    truncated = jnp.mod(horizon - 1 - horizon_offset - here * steps, horizon)
    times = jnp.concatenate([done_steps.T - here * steps, truncated[None]], axis=0)
    segments, whole = summary(rewards, values, times, rates)

    val_2, val_1 = exchange(pack(values, blocks, quarter, quarter, whole), val_1)
    val_3, val_2 = exchange(pack(values, blocks, half, half), val_2)
    every = val_2[:, rows(quarter) :, :]
    adv, local = advantage(
        here.reshape(1), rewards, values, times, rates, last_value[None], segments, every
    )
    adv_1, val_3 = exchange(pack(adv, blocks, 0, half, local), val_3)
    adv_2, adv_1 = exchange(pack(adv, blocks, half, half), adv_1)

    parts = adv_1[:, rows(half), : 4 * groups].reshape(-1, 4)
    count = float(steps * LANES)
    means = parts[:, :2] / count
    mean = jnp.mean(means, axis=0)
    off = means - mean
    square = jnp.sum(parts[:, 2:] + count * off * off, axis=0)
    count = count * groups * blocks
    mean, square, count = merged(mean, square, count, ENV[1], 1)
    mean, square, count = merged(mean, square, count, ENV[0], 1)
    mean, square, count = merged(mean, square, count, ENV[0], 2)
    scale = 1.0 / jnp.sqrt(square / count + 1e-05)
    stats = jnp.stack([mean[0], scale[0], mean[1], scale[1]])

    counts = (rows(quarter), rows(quarter))
    out = normalized(stats, adv_1, (val_1, val_2), counts, own, steps, 0)
    return tuple(normalized(stats, adv_2, (val_3,), (rows(half),), own, steps, half, out))


def solution(mesh):
    split = Mesh(mesh.devices.reshape(4, 4, 4, 2), ALL)
    placed = (P(TM, ENV), P(TM, ENV), P(ENV), P(ENV, None), P(ENV), P(ENV), P(ENV))
    return jax.shard_map(
        shards,
        mesh=split,
        in_specs=placed,
        out_specs=(P(ENV_TM, None), P(ENV_TM, None)),
        check_vma=False,
    )
```

time: 454 us -> 156 us (0.34)
  the two profiles are of different devices: /device:TPU:114 before, /device:TPU:0 now
where the time goes in v1:
time: 156 us; the launch traced here: 155 us
  waiting for transfers between devices  60.9 us (39%)
  Pallas kernels  56.7 us (36%)
  starting transfers between devices  29 us (19%)
  other arithmetic  4.99 us (3%)
  local copies, waits for them, and re-layouts  2.76 us (2%)
    all_to_all x5, waiting for transfers between devices, exchange(): return (lax.all_to_all(packed, TM, 0, 0, tiled=True), behind)  53.3 us
    all_to_all x5, starting transfers between devices, exchange(): return (lax.all_to_all(packed, TM, 0, 0, tiled=True), behind)  25.7 us
    pallas_call x1, Pallas kernels, advantage(): pl.pallas_call(functools.partial(advantage_body, steps // SEG), grid=(env...  17.4 us
    pallas_call x5, Pallas kernels, pack(): pl.pallas_call(functools.partial(pack_body, dests, riders), grid=(count /...  17.3 us
    pallas_call x1, Pallas kernels, summary(): pl.pallas_call(functools.partial(summary_body, steps // SEG), grid=(group...  11.7 us
    pallas_call x2, Pallas kernels, normalized(): pl.pallas_call(functools.partial(normal_body, counts, steps, offset), in_...  10.3 us
    ppermute x3, waiting for transfers between devices, merged(): lax.ppermute(jnp.concatenate([mean, square]), axis, [(i, (i + distance) %...  7.6 us
    ppermute x3, starting transfers between devices, merged(): lax.ppermute(jnp.concatenate([mean, square]), axis, [(i, (i + distance) %...  3.34 us
  transfers between devices with their start and end apart: 8, of which 8 were waited for; matrix products, arithmetic and copies ran while one was open for 4% of the time, Pallas kernels for 32%

profile of v1, /device:TPU:0, one launch (start us, length us, event | category | flops | bytes accessed | tf_op | source)
XLA Modules:
  0.0 155.1 jit_solution(3280731312981240538)
XLA Ops:
  0.7 2.3 %pack.7 = f32[16,128,128]{2,1,0:T(8,128)} custom-call(f32[2048,512]{1,0:T(8,128)} %val_ref.3), custom_call_target="tpu_custom_call" | custom-call | bytes 2097152 | tf_op jit(solution)/shard_map/pack/pallas_call | solution.py:63
  2.9 8.1 %all-to-all-start = ((f32[16,128,128]{2,1,0:T(8,128)}), f32[16,128,128]{2,1,0:T(8,128)S(1)}, u32[]{:S(2)}, u32[]{:S(2)}) async-start(f32[16,128,128]{2,1,0:T(8,128)} %pack.7), calls=%async_computation | async-start | bytes 2097152 | tf_op jit(solution)/shard_map/all_to_all | solution.py:325
  12.4 11.7 %summary.1 = (f32[3,32,512]{2,1,0:T(8,128)}, f32[16,128]{1,0:T(8,128)}) custom-call(f32[2048,512]{1,0:T(8,128)} %rew_ref.3, f32[2048,512]{1,0:T(8,128)} %val_ref.3, s32[5,512]{1,0:T(8,128)} %pad_add_fusion.times_ref, f32[2,512]{1,0:T(2,128)} %pad_maximum_fusion.rates_ref), custom_call_target="tpu_custom_call" | custom-call | flops 16777216 | bytes 8388608 | tf_op jit(solution)/shard_map/summary/pallas_call | solution.py:143
  24.0 2.5 %pack.6 = f32[16,144,128]{2,1,0:T(8,128)} custom-call(f32[2048,512]{1,0:T(8,128)} %val_ref.3, f32[16,128]{1,0:T(8,128)} %get-tuple-element.17.refs_1_), custom_call_target="tpu_custom_call" | custom-call | bytes 2097152 | tf_op jit(solution)/shard_map/pack/pallas_call | solution.py:63
  26.5 2.2 %all-to-all-done.refs_0_ = f32[16,128,128]{2,1,0:T(8,128)S(1)} async-done(((f32[16,128,128]{2,1,0:T(8,128)}), f32[16,128,128]{2,1,0:T(8,128)S(1)}, u32[]{:S(2)}, u32[]{:S(2)}) %all-to-all-start) | async-done | bytes 1048608 | tf_op jit(solution)/shard_map/all_to_all | solution.py:325
  28.8 5.0 %all-to-all-start.1 = ((f32[16,144,128]{2,1,0:T(8,128)}), f32[16,144,128]{2,1,0:T(8,128)S(1)}, u32[]{:S(2)}, u32[]{:S(2)}) async-start(f32[16,144,128]{2,1,0:T(8,128)} %pack.6), calls=%async_computation.1 | async-start | bytes 2359296 | tf_op jit(solution)/shard_map/all_to_all | solution.py:325
  33.8 4.2 %pack.5 = f32[16,256,128]{2,1,0:T(8,128)} custom-call(f32[2048,512]{1,0:T(8,128)} %val_ref.3), custom_call_target="tpu_custom_call" | custom-call | bytes 4194304 | tf_op jit(solution)/shard_map/pack/pallas_call | solution.py:63
  38.0 14.3 %all-to-all-done.1.refs_1_ = f32[16,144,128]{2,1,0:T(8,128)S(1)} async-done(((f32[16,144,128]{2,1,0:T(8,128)}), f32[16,144,128]{2,1,0:T(8,128)S(1)}, u32[]{:S(2)}, u32[]{:S(2)}) %all-to-all-start.1) | async-done | bytes 1179680 | tf_op jit(solution)/shard_map/all_to_all | solution.py:325
  52.3 3.7 %all-to-all-start.2 = ((f32[16,256,128]{2,1,0:T(8,128)}), f32[16,256,128]{2,1,0:T(8,128)S(1)}, u32[]{:S(2)}, u32[]{:S(2)}) async-start(f32[16,256,128]{2,1,0:T(8,128)} %pack.5), calls=%async_computation.2 | async-start | bytes 4194304 | tf_op jit(solution)/shard_map/all_to_all | solution.py:325
  56.7 17.4 %advantage.1 = (f32[2048,512]{1,0:T(8,128)}, f32[8,128]{1,0:T(8,128)}) custom-call(s32[1]{0:T(128)} %bitcast.here_ref, f32[2048,512]{1,0:T(8,128)} %rew_ref.3, f32[2048,512]{1,0:T(8,128)} %val_ref.3, s32[5,512]{1,0:T(8,128)} %pad_add_fusion.times_ref, f32[2,512]{1,0:T(2,128)} %pad_maximum_fusion.rates_ref, f32[1,512]{1,0:T(1,128)} %bitcast.10, ...), custom_call_target="tpu_custom_call" | custom-call | flops 25165824 | bytes 12582912 | tf_op jit(solution)/shard_map/advantage/pallas_call | solution.py:224
  74.1 4.1 %pack.9 = f32[16,264,128]{2,1,0:T(8,128)} custom-call(f32[2048,512]{1,0:T(8,128)} %get-tuple-element.20.refs_0_, f32[8,128]{1,0:T(8,128)} %get-tuple-element.21.refs_1_), custom_call_target="tpu_custom_call" | custom-call | bytes 4194304 | tf_op jit(solution)/shard_map/pack/pallas_call | solution.py:63
  78.2 5.6 %all-to-all-done.2.refs_0_ = f32[16,256,128]{2,1,0:T(8,128)S(1)} async-done(((f32[16,256,128]{2,1,0:T(8,128)}), f32[16,256,128]{2,1,0:T(8,128)S(1)}, u32[]{:S(2)}, u32[]{:S(2)}) %all-to-all-start.2) | async-done | bytes 2097184 | tf_op jit(solution)/shard_map/all_to_all | solution.py:325
  85.1 4.3 %all-to-all-start.3 = ((f32[16,264,128]{2,1,0:T(8,128)}), f32[16,264,128]{2,1,0:T(8,128)S(1)}, u32[]{:S(2)}, u32[]{:S(2)}) async-start(f32[16,264,128]{2,1,0:T(8,128)} %pack.9), calls=%async_computation.3 | async-start | bytes 4325376 | tf_op jit(solution)/shard_map/all_to_all | solution.py:325
  89.4 4.2 %pack.8 = f32[16,256,128]{2,1,0:T(8,128)} custom-call(f32[2048,512]{1,0:T(8,128)} %get-tuple-element.20.refs_0_), custom_call_target="tpu_custom_call" | custom-call | bytes 4194304 | tf_op jit(solution)/shard_map/pack/pallas_call | solution.py:63
  93.6 24.2 %all-to-all-done.3.adv = f32[16,264,128]{2,1,0:T(8,128)S(1)} async-done(((f32[16,264,128]{2,1,0:T(8,128)}), f32[16,264,128]{2,1,0:T(8,128)S(1)}, u32[]{:S(2)}, u32[]{:S(2)}) %all-to-all-start.3) | async-done | bytes 2162720 | tf_op jit(solution)/shard_map/all_to_all | solution.py:325
  117.8 4.6 %all-to-all-start.4 = ((f32[16,256,128]{2,1,0:T(8,128)}), f32[16,256,128]{2,1,0:T(8,128)}, u32[]{:S(2)}, u32[]{:S(2)}) async-start(f32[16,256,128]{2,1,0:T(8,128)} %pack.8), calls=%async_computation.4 | async-start | bytes 4194304 | tf_op jit(solution)/shard_map/all_to_all | solution.py:325
  124.0 1.5 collective-permute-start.1
  125.5 3.3 %collective-permute-done.1 = f32[4]{0:T(128)S(1)} collective-permute-done((f32[4]{0:T(128)S(1)}, f32[4]{0:T(128)S(1)}, u32[]{:S(2)}, u32[]{:S(2)}) %collective-permute-start.1) | collective-permute-done | bytes 48 | tf_op jit(solution)/shard_map/ppermute | solution.py:330
  128.9 1.8 %collective-permute-start.2 = (f32[4]{0:T(128)S(1)}, f32[4]{0:T(128)S(1)}, u32[]{:S(2)}, u32[]{:S(2)}) collective-permute-start(f32[4]{0:T(128)S(1)} %pad_maximum_fusion.3), channel_id=1, source_target_pairs={{0,4},{2,6},{4,0},{6,2},{1,5},{3,7},{5,1},{7,3},{8,12},{10,14},{12... | collective-permute-start | bytes 56 | tf_op jit(solution)/shard_map/ppermute | solution.py:330
  130.7 3.2 %collective-permute-done.2 = f32[4]{0:T(128)S(1)} collective-permute-done((f32[4]{0:T(128)S(1)}, f32[4]{0:T(128)S(1)}, u32[]{:S(2)}, u32[]{:S(2)}) %collective-permute-start.2) | collective-permute-done | bytes 48 | tf_op jit(solution)/shard_map/ppermute | solution.py:330
  134.7 3.2 %pad_maximum_fusion.4.stat_ref = f32[4]{0:T(128)} fusion(f32[1]{0:T(128)} %get-tuple-element.42, f32[1]{0:T(128)} %get-tuple-element.39, f32[1]{0:T(128)} %get-tuple-element.43, f32[1]{0:T(128)} %get-tuple-element.38), kind=kLoop, calls=%fused_computation.24 | loop fusion | flops 12 | bytes 32 | tf_op jit(solution)/shard_map/stack | solution.py:375
  137.9 5.3 %normalized.2 = (f32[32,32768]{1,0:T(8,128)}, f32[32,32768]{1,0:T(8,128)}) custom-call(f32[4]{0:T(128)} %pad_maximum_fusion.4.stat_ref, f32[16,264,128]{2,1,0:T(8,128)} %copy-done, f32[16,128,128]{2,1,0:T(8,128)} %copy-done.3, f32[16,144,128]{2,1,0:T(8,128)} %copy-done.2), custom_call_target="tpu_custom_call" | custom-call | flops 2097152 | bytes 8388608 | tf_op jit(solution)/shard_map/normalized/pallas_call | solution.py:302
  143.1 6.9 %all-to-all-done.4.adv = f32[16,256,128]{2,1,0:T(8,128)} async-done(((f32[16,256,128]{2,1,0:T(8,128)}), f32[16,256,128]{2,1,0:T(8,128)}, u32[]{:S(2)}, u32[]{:S(2)}) %all-to-all-start.4) | async-done | bytes 2097184 | tf_op jit(solution)/shard_map/all_to_all | solution.py:325
  150.1 5.1 %normalized.3 = (f32[32,32768]{1,0:T(8,128)}, f32[32,32768]{1,0:T(8,128)}) custom-call(f32[4]{0:T(128)} %pad_maximum_fusion.4.stat_ref, f32[16,256,128]{2,1,0:T(8,128)} %all-to-all-done.4.adv, f32[16,256,128]{2,1,0:T(8,128)} %copy-done.1, f32[32,32768]{1,0:T(8,128)} %get-tuple-element.28.refs_1_, ...), custom_call_target="tpu_custom_call", output_to_operand_aliasing={{0}: (3, {}), {1}: (4, {})} | custom-call | flops 2097152 | bytes 8388608 | tf_op jit(solution)/shard_map/normalized/pallas_call | solution.py:302
  (36 shorter events, 5.7 us)
Async XLA Ops:
  0.6 10.5 %copy-start.7 = (f32[512]{0:T(512)S(1)}, f32[512]{0:T(512)}, u32[]{:S(2)}) copy-start(f32[512]{0:T(512)} %param.13) | copy-start | bytes 6148
  0.6 10.5 %copy-start.6 = (f32[512]{0:T(512)S(1)}, f32[512]{0:T(512)}, u32[]{:S(2)}) copy-start(f32[512]{0:T(512)} %param.12) | copy-start | bytes 6148
  0.7 11.1 %copy-start.5 = (s32[512]{0:T(512)S(1)}, s32[512]{0:T(512)}, u32[]{:S(2)}) copy-start(s32[512]{0:T(512)} %param.11) | copy-start | bytes 6148
  0.7 11.1 %copy-start.4 = (s32[512,4]{0,1:T(4,128)S(1)}, s32[512,4]{0,1:T(4,128)}, u32[]{:S(2)}) copy-start(s32[512,4]{0,1:T(4,128)} %param.10) | copy-start | bytes 24580
  2.9 25.8 %all-to-all-start = ((f32[16,128,128]{2,1,0:T(8,128)}), f32[16,128,128]{2,1,0:T(8,128)S(1)}, u32[]{:S(2)}, u32[]{:S(2)}) async-start(f32[16,128,128]{2,1,0:T(8,128)} %pack.7), calls=%async_computation | async-start | bytes 2097152 | tf_op jit(solution)/shard_map/all_to_all | solution.py:325
  28.8 9.2 %copy-start.3 = (f32[16,128,128]{2,1,0:T(8,128)}, f32[16,128,128]{2,1,0:T(8,128)S(1)}, u32[]{:S(2)}) copy-start(f32[16,128,128]{2,1,0:T(8,128)S(1)} %all-to-all-done.refs_0_) | copy-start | bytes 3145732
  28.8 23.5 %all-to-all-start.1 = ((f32[16,144,128]{2,1,0:T(8,128)}), f32[16,144,128]{2,1,0:T(8,128)S(1)}, u32[]{:S(2)}, u32[]{:S(2)}) async-start(f32[16,144,128]{2,1,0:T(8,128)} %pack.6), calls=%async_computation.1 | async-start | bytes 2359296 | tf_op jit(solution)/shard_map/all_to_all | solution.py:325
  52.3 4.4 %copy-start.2 = (f32[16,144,128]{2,1,0:T(8,128)}, f32[16,144,128]{2,1,0:T(8,128)S(1)}, u32[]{:S(2)}) copy-start(f32[16,144,128]{2,1,0:T(8,128)S(1)} %all-to-all-done.1.refs_1_) | copy-start | bytes 3538948
  52.3 31.5 %all-to-all-start.2 = ((f32[16,256,128]{2,1,0:T(8,128)}), f32[16,256,128]{2,1,0:T(8,128)S(1)}, u32[]{:S(2)}, u32[]{:S(2)}) async-start(f32[16,256,128]{2,1,0:T(8,128)} %pack.5), calls=%async_computation.2 | async-start | bytes 4194304 | tf_op jit(solution)/shard_map/all_to_all | solution.py:325
  83.8 1.3 copy-start.1
  85.1 32.7 %all-to-all-start.3 = ((f32[16,264,128]{2,1,0:T(8,128)}), f32[16,264,128]{2,1,0:T(8,128)S(1)}, u32[]{:S(2)}, u32[]{:S(2)}) async-start(f32[16,264,128]{2,1,0:T(8,128)} %pack.9), calls=%async_computation.3 | async-start | bytes 4325376 | tf_op jit(solution)/shard_map/all_to_all | solution.py:325
  117.8 4.8 %copy-start = (f32[16,264,128]{2,1,0:T(8,128)}, f32[16,264,128]{2,1,0:T(8,128)S(1)}, u32[]{:S(2)}) copy-start(f32[16,264,128]{2,1,0:T(8,128)S(1)} %all-to-all-done.3.adv) | copy-start | bytes 6488068
  117.8 32.3 %all-to-all-start.4 = ((f32[16,256,128]{2,1,0:T(8,128)}), f32[16,256,128]{2,1,0:T(8,128)}, u32[]{:S(2)}, u32[]{:S(2)}) async-start(f32[16,256,128]{2,1,0:T(8,128)} %pack.8), calls=%async_computation.4 | async-start | bytes 4194304 | tf_op jit(solution)/shard_map/all_to_all | solution.py:325
  122.7 1.1 collective-permute-start
  124.0 4.8 %collective-permute-start.1 = (f32[4]{0:T(128)S(1)}, f32[4]{0:T(128)S(1)}, u32[]{:S(2)}, u32[]{:S(2)}) collective-permute-start(f32[4]{0:T(128)S(1)} %pad_maximum_fusion.2), channel_id=1, source_target_pairs={{0,2},{2,4},{4,6},{6,0},{1,3},{3,5},{5,7},{7,1},{8,10},{10,12},{12... | collective-permute-start | bytes 56 | tf_op jit(solution)/shard_map/ppermute | solution.py:330
  128.9 5.1 %collective-permute-start.2 = (f32[4]{0:T(128)S(1)}, f32[4]{0:T(128)S(1)}, u32[]{:S(2)}, u32[]{:S(2)}) collective-permute-start(f32[4]{0:T(128)S(1)} %pad_maximum_fusion.3), channel_id=1, source_target_pairs={{0,4},{2,6},{4,0},{6,2},{1,5},{3,7},{5,1},{7,3},{8,12},{10,14},{12... | collective-permute-start | bytes 56 | tf_op jit(solution)/shard_map/ppermute | solution.py:330

commit v2 on v1

--- a/solution.py
+++ b/solution.py
@@ -72,50 +72,53 @@
     )(block, *(() if rider is None else (rider,)))
 
 
-def stepper(rew_ref, val_ref, times_ref, rates_ref, length):
+def stepper(times_ref, rates_ref, length):
     first = lax.broadcasted_iota(jnp.int32, (SEG, LANES), 0) * length
-    marks = [
-        jnp.broadcast_to(times_ref[k : k + 1, :], (8, LANES))
-        for k in range(times_ref.shape[0])
-    ]
-    marks = [jnp.concatenate([m] * (SEG // 8), axis=0) for m in marks]
-    discount = jnp.broadcast_to(rates_ref[0:1, :], (SEG, LANES))
-    retention = jnp.broadcast_to(rates_ref[1:2, :], (SEG, LANES))
-
-    def step(i, next_value):
-        rows = pl.ds(i, SEG, stride=length)
-        reward, value = rew_ref[rows, :], val_ref[rows, :]
+    marks = [times_ref[k : k + 1, :] for k in range(times_ref.shape[0])]
+    discount, retention = rates_ref[0:1, :], rates_ref[1:2, :]
+
+    def step(i, reward, value, next_value):
         time = first + i
         ended = marks[0] == time
         for mark in marks[1:-1]:
             ended = ended | (mark == time)
         follow = jnp.where(ended, 0.0, discount)
         decay = jnp.where(ended | (marks[-1] == time), 0.0, retention)
-        td_error = reward + follow * next_value - value
-        return value, td_error, decay, follow
+        return reward + follow * next_value - value, decay, follow
 
     return step
 
 
-def value_after(val_ref, boundary, length):
-    firsts = val_ref[pl.ds(0, SEG, stride=length), :]
+def by_step(ref, at):
+    return jnp.swapaxes(ref[:, pl.ds(pl.multiple_of(at, 8), 8), :], 0, 1)
+
+
+def value_after(val_ref, boundary):
+    firsts = jnp.swapaxes(val_ref[:, 0:8, :], 0, 1)[0]
     return jnp.concatenate([firsts[1:], boundary], axis=0)
 
 
-def summary_body(length, rew_ref, val_ref, times_ref, rates_ref, seg_ref, all_ref):
-    step = stepper(rew_ref, val_ref, times_ref, rates_ref, length)
+def summary_body(rew_ref, val_ref, times_ref, rates_ref, seg_ref, all_ref):
+    length = rew_ref.shape[1]
+    step = stepper(times_ref, rates_ref, length)
     zero = jnp.zeros((SEG, LANES), F32)
 
-    following = value_after(val_ref, zero[:1], length)
-    value, partial, last_decay, last_follow = step(length - 1, following)
-
-    def body(k, carry):
-        partial, product, following = carry
-        value, td_error, decay, _ = step(length - 2 - k, following)
-        return td_error + decay * partial, decay * product, value
-
-    partial, product, _ = lax.fori_loop(
-        0, length - 1, body, (partial, zero + 1.0, value), unroll=7
+    def eight(at, partial, product, following, last):
+        rewards, values = by_step(rew_ref, at), by_step(val_ref, at)
+        for k in range(7, -1, -1):
+            td_error, decay, follow = step(at + k, rewards[k], values[k], following)
+            if last and k == 7:
+                partial, kept = td_error, (decay, follow)
+            else:
+                partial, product = td_error + decay * partial, decay * product
+            following = values[k]
+        return (partial, product, following), (kept if last else None)
+
+    carry, (last_decay, last_follow) = eight(
+        length - 8, zero, zero + 1.0, value_after(val_ref, zero[:1]), True
+    )
+    partial, product, following = lax.fori_loop(
+        1, length // 8, lambda k, c: eight(length - 8 - 8 * k, *c, False)[0], carry
     )
     coefs = product * last_follow
     product = product * last_decay
@@ -129,21 +132,28 @@
         own = partial[s : s + 1] + factor * own
         kept = factor * kept
         coef = factor * coef
-    lines = jnp.concatenate([own, kept, coef, val_ref[0:1, :]], axis=0)
+    lines = jnp.concatenate([own, kept, coef, following[0:1]], axis=0)
     all_ref[pl.ds(4 * pl.program_id(0), 4), :] = lines
 
 
 def columns(*lead):
     return pl.BlockSpec((*lead, LANES), lambda j: (*(0 for _ in lead), j))
+
+
+def segmented(block):
+    steps, envs = block.shape
+    return block.reshape(SEG, steps // SEG, envs)
 
 
 def summary(rewards, values, times, rates):
     steps, envs = rewards.shape
     groups = envs // LANES
     return pl.pallas_call(
-        functools.partial(summary_body, steps // SEG),
+        summary_body,
         grid=(groups,),
-        in_specs=[columns(steps), columns(steps), columns(len(times)), columns(2)],
+        in_specs=[
+            columns(SEG, steps // SEG), columns(SEG, steps // SEG), columns(len(times)), columns(2),
+        ],
         out_specs=[columns(3, SEG), pl.BlockSpec((4 * groups, LANES), lambda j: (0, 0))],
         out_shape=[
             jax.ShapeDtypeStruct((3, SEG, envs), F32),
@@ -152,16 +162,16 @@
         compiler_params=params(),
         cost_estimate=cost(16 * steps * envs, 8 * steps * envs),
         name="summary",
-    )(rewards, values, times, rates)
+    )(segmented(rewards), segmented(values), times, rates)
 
 
 def advantage_body(
-    length, here_ref, rew_ref, val_ref, times_ref, rates_ref, last_ref, seg_ref, every_ref, adv_ref, stat_ref
+    here_ref, rew_ref, val_ref, times_ref, rates_ref, last_ref, seg_ref, every_ref, adv_ref, stat_ref
 ):
-    steps = rew_ref.shape[0]
+    length = rew_ref.shape[1]
     group = pl.program_id(0)
     here = here_ref[0]
-    step = stepper(rew_ref, val_ref, times_ref, rates_ref, length)
+    step = stepper(times_ref, rates_ref, length)
 
     boundary = last_ref[...]
     incoming = jnp.zeros((1, LANES), F32)
@@ -183,29 +193,35 @@
 
     def body(k, carry):
         later, following, sum_adv, sum_val = carry
-        i = length - 1 - k
-        value, td_error, decay, _ = step(i, following)
-        own = td_error + decay * later
-        adv_ref[pl.ds(i, SEG, stride=length), :] = own
-        return own, value, sum_adv + own, sum_val + value
+        at = length - 8 - 8 * k
+        rewards, values = by_step(rew_ref, at), by_step(val_ref, at)
+        found = []
+        for k in range(7, -1, -1):
+            td_error, decay, _ = step(at + k, rewards[k], values[k], following)
+            later = td_error + decay * later
+            following = values[k]
+            found.append(later)
+            sum_adv, sum_val = sum_adv + later, sum_val + following
+        found = jnp.stack(found[::-1], axis=0)
+        adv_ref[:, pl.ds(pl.multiple_of(at, 8), 8), :] = jnp.swapaxes(found, 0, 1)
+        return later, following, sum_adv, sum_val
 
     zero = jnp.zeros((SEG, LANES), F32)
-    start = (after, value_after(val_ref, boundary, length), zero, zero)
-    _, _, sum_adv, sum_val = lax.fori_loop(0, length, body, start, unroll=8)
+    start = (after, value_after(val_ref, boundary), zero, zero)
+    _, _, sum_adv, sum_val = lax.fori_loop(0, length // 8, body, start)
     sums = [jnp.sum(sum_adv), jnp.sum(sum_adv + sum_val)]
-    mean_adv, mean_ret = [total / (steps * LANES) for total in sums]
-
-    zero = jnp.zeros((64, LANES), F32)
+    mean_adv, mean_ret = [total / (SEG * length * LANES) for total in sums]
+
+    zero = jnp.zeros((length, LANES), F32)
 
     def spread(k, carry):
         sq_adv, sq_ret = carry
-        rows = pl.ds(pl.multiple_of(k * 64, 64), 64)
-        own = adv_ref[rows, :]
+        own = adv_ref[k]
         off_adv = own - mean_adv
-        off_ret = (own + val_ref[rows, :]) - mean_ret
+        off_ret = (own + val_ref[k]) - mean_ret
         return sq_adv + off_adv * off_adv, sq_ret + off_ret * off_ret
 
-    sq_adv, sq_ret = lax.fori_loop(0, steps // 64, spread, (zero, zero), unroll=2)
+    sq_adv, sq_ret = lax.fori_loop(0, SEG, spread, (zero, zero), unroll=2)
     sums += [jnp.sum(sq_adv), jnp.sum(sq_ret)]
     lane = lax.broadcasted_iota(jnp.int32, stat_ref.shape, 1)
 
@@ -221,22 +237,23 @@
 
 def advantage(here, rewards, values, times, rates, last_value, segments, every):
     steps, envs = rewards.shape
-    return pl.pallas_call(
-        functools.partial(advantage_body, steps // SEG),
+    adv, stats = pl.pallas_call(
+        advantage_body,
         grid=(envs // LANES,),
         in_specs=[
-            SMEM, columns(steps), columns(steps), columns(len(times)), columns(2), columns(1),
-            columns(3, SEG), pl.BlockSpec(every.shape, lambda j: (0, 0, 0)),
+            SMEM, columns(SEG, steps // SEG), columns(SEG, steps // SEG), columns(len(times)),
+            columns(2), columns(1), columns(3, SEG), pl.BlockSpec(every.shape, lambda j: (0, 0, 0)),
         ],
-        out_specs=[columns(steps), pl.BlockSpec((8, LANES), lambda j: (0, 0))],
+        out_specs=[columns(SEG, steps // SEG), pl.BlockSpec((8, LANES), lambda j: (0, 0))],
         out_shape=[
-            jax.ShapeDtypeStruct((steps, envs), F32),
+            jax.ShapeDtypeStruct((SEG, steps // SEG, envs), F32),
             jax.ShapeDtypeStruct((8, LANES), F32),
         ],
         compiler_params=params(),
         cost_estimate=cost(24 * steps * envs, 12 * steps * envs),
         name="advantage",
-    )(here, rewards, values, times, rates, last_value, segments, every)
+    )(here, segmented(rewards), segmented(values), times, rates, last_value, segments, every)
+    return adv.reshape(steps, envs), stats
 
 
 def normal_body(counts, steps, offset, stat_ref, adv, *refs):
@@ -344,13 +361,24 @@
     half, quarter = steps // 2, steps // 4
     rows = lambda count: count // LANES * own
 
-    val_1, _ = exchange(pack(values, blocks, 0, quarter))
-
     discount = jnp.exp(-discount_rate)
     rates = jnp.stack([discount, discount * jnp.exp(-trace_rate)])
     truncated = jnp.mod(horizon - 1 - horizon_offset - here * steps, horizon)
     times = jnp.concatenate([done_steps.T - here * steps, truncated[None]], axis=0)
-    segments, whole = summary(rewards, values, times, rates)
+
+    core = lax.axis_index(ENV[1])
+    given = (rewards, values, times, rates)
+    blank = lambda *_: (
+        jnp.zeros((3, SEG, envs), F32),
+        jnp.zeros((4 * groups, LANES), F32),
+    )
+    ahead = lax.cond(core == 0, lambda *x: tuple(summary(*x)), blank, *given)
+    values_1, ahead = lax.optimization_barrier((values, ahead))
+    packed, ahead = lax.optimization_barrier((pack(values_1, blocks, 0, quarter), ahead))
+    val_1, _ = exchange(packed)
+    segments, whole = lax.cond(
+        core == 0, lambda done, *_: done, lambda _, *x: tuple(summary(*x)), ahead, *given
+    )
 
     val_2, val_1 = exchange(pack(values, blocks, quarter, quarter, whole), val_1)
     val_3, val_2 = exchange(pack(values, blocks, half, half), val_2)

time: 156 us -> 133 us (0.85)
  waiting for transfers between devices: 60.9 us -> 47.7 us
  Pallas kernels: 56.7 us -> 44.1 us
  starting transfers between devices: 29 us -> 31.1 us
    all_to_all x5, waiting for transfers between devices: 53.3 us -> 40.1 us  [exchange(): return (lax.all_to_all(packed, TM, 0, 0, tiled=True), behind)]
    pallas_call x2, Pallas kernels: 29.1 us -> 16.6 us  [the longest x1 10.3 us: advantage(): pl.pallas_call(advantage_body, grid=(envs // LANES,), in_specs=[SMEM, col...]
    all_to_all x5, starting transfers between devices: 25.7 us -> 27.7 us  [exchange(): return (lax.all_to_all(packed, TM, 0, 0, tiled=True), behind)]
  transfers between devices with their start and end apart: 8 -> 8, of which waited for: 8 -> 7; matrix products, arithmetic and copies ran while one was open for 4% -> 4% of each run, Pallas kernels for 32% -> 23%
where the time goes in v2:
time: 133 us; the launch traced here: 132 us
  waiting for transfers between devices  47.7 us (36%)
  Pallas kernels  44.1 us (33%)
  starting transfers between devices  31.1 us (23%)
  other arithmetic  5.85 us (4%)
  local copies, waits for them, and re-layouts  2.67 us (2%)
    all_to_all x5, waiting for transfers between devices, exchange(): return (lax.all_to_all(packed, TM, 0, 0, tiled=True), behind)  40.1 us
    all_to_all x5, starting transfers between devices, exchange(): return (lax.all_to_all(packed, TM, 0, 0, tiled=True), behind)  27.7 us
    pallas_call x5, Pallas kernels, pack(): pl.pallas_call(functools.partial(pack_body, dests, riders), grid=(count /...  17.2 us
    pallas_call x2, Pallas kernels, normalized(): pl.pallas_call(functools.partial(normal_body, counts, steps, offset), in_...  10.3 us
    pallas_call x1, Pallas kernels, advantage(): pl.pallas_call(advantage_body, grid=(envs // LANES,), in_specs=[SMEM, col...  10.3 us
    ppermute x3, waiting for transfers between devices, merged(): lax.ppermute(jnp.concatenate([mean, square]), axis, [(i, (i + distance) %...  7.6 us
    pallas_call x1, Pallas kernels, summary(): pl.pallas_call(summary_body, grid=(groups,), in_specs=[columns(SEG, steps...  6.34 us
    ppermute x3, starting transfers between devices, merged(): lax.ppermute(jnp.concatenate([mean, square]), axis, [(i, (i + distance) %...  3.34 us
  transfers between devices with their start and end apart: 8, of which 7 were waited for; matrix products, arithmetic and copies ran while one was open for 4% of the time, Pallas kernels for 23%

profile of v2, /device:TPU:0, one launch (start us, length us, event | category | flops | bytes accessed | tf_op | source)
XLA Modules:
  0.0 132.2 jit_solution(5672083265109887436)
XLA Ops:
  2.8 6.4 %conditional.2 = ((f32[3,32,512]{2,1,0:T(8,128)S(1)}, f32[16,128]{1,0:T(8,128)S(1)})) conditional(s32[]{:T(128)} %convert_element_type.4, () %tuple.27, (f32[2048,512]{1,0:T(8,128)}, f32[2048,512]{1,0:T(8,128)}, s32[5,512]{1,0:T(8,128)S(1)}, f32[2,512]{1,0:T(2,128)S(1)}) %tuple.26), branch_computations={%region_0.1_spmd, %region_1.2_spmd} | conditional | flops 16777216 | bytes 8388616 | solution.py:375
  2.8 6.3 %summary.2 = (f32[3,32,512]{2,1,0:T(8,128)S(1)}, f32[16,128]{1,0:T(8,128)S(1)}) custom-call(f32[32,64,512]{2,1,0:T(8,128)} %bitcast.18, f32[32,64,512]{2,1,0:T(8,128)} %bitcast.15, s32[5,512]{1,0:T(8,128)S(1)} %get-tuple-element.22.times_ref, f32[2,512]{1,0:T(2,128)S(1)} %get-tuple-element.23.rates_ref), custom_call_target="tpu_custom_call" | custom-call | flops 16777216 | bytes 8388608 | tf_op jit(solution)/shard_map/cond/branch_1_fun/summary/pallas_call | solution.py:151
  9.1 2.3 %pack.5 = f32[16,128,128]{2,1,0:T(8,128)} custom-call(f32[2048,512]{1,0:T(8,128)} %refs_0_.4), custom_call_target="tpu_custom_call" | custom-call | bytes 2097152 | tf_op jit(solution)/shard_map/pack/pallas_call | solution.py:63
  11.4 8.1 %all-to-all-start = ((f32[16,128,128]{2,1,0:T(8,128)}), f32[16,128,128]{2,1,0:T(8,128)S(1)}, u32[]{:S(2)}, u32[]{:S(2)}) async-start(f32[16,128,128]{2,1,0:T(8,128)} %pack.5), calls=%async_computation | async-start | bytes 2097152 | tf_op jit(solution)/shard_map/all_to_all | solution.py:342
  19.6 2.5 %pack.7 = f32[16,144,128]{2,1,0:T(8,128)} custom-call(f32[2048,512]{1,0:T(8,128)} %refs_0_.4, f32[16,128]{1,0:T(8,128)S(1)} %get-tuple-element.60.refs_1_), custom_call_target="tpu_custom_call" | custom-call | bytes 2097152 | tf_op jit(solution)/shard_map/pack/pallas_call | solution.py:63
  22.1 10.4 %all-to-all-done.refs_0_ = f32[16,128,128]{2,1,0:T(8,128)S(1)} async-done(((f32[16,128,128]{2,1,0:T(8,128)}), f32[16,128,128]{2,1,0:T(8,128)S(1)}, u32[]{:S(2)}, u32[]{:S(2)}) %all-to-all-start) | async-done | bytes 1048608 | tf_op jit(solution)/shard_map/all_to_all | solution.py:342
  32.5 3.7 %all-to-all-start.1 = ((f32[16,144,128]{2,1,0:T(8,128)}), f32[16,144,128]{2,1,0:T(8,128)S(1)}, u32[]{:S(2)}, u32[]{:S(2)}) async-start(f32[16,144,128]{2,1,0:T(8,128)} %pack.7), calls=%async_computation.1 | async-start | bytes 2359296 | tf_op jit(solution)/shard_map/all_to_all | solution.py:342
  36.2 4.1 %pack.6 = f32[16,256,128]{2,1,0:T(8,128)} custom-call(f32[2048,512]{1,0:T(8,128)} %refs_0_.4), custom_call_target="tpu_custom_call" | custom-call | bytes 4194304 | tf_op jit(solution)/shard_map/pack/pallas_call | solution.py:63
  40.3 9.6 %all-to-all-done.1.refs_1_ = f32[16,144,128]{2,1,0:T(8,128)S(1)} async-done(((f32[16,144,128]{2,1,0:T(8,128)}), f32[16,144,128]{2,1,0:T(8,128)S(1)}, u32[]{:S(2)}, u32[]{:S(2)}) %all-to-all-start.1) | async-done | bytes 1179680 | tf_op jit(solution)/shard_map/all_to_all | solution.py:342
  49.9 3.7 %all-to-all-start.2 = ((f32[16,256,128]{2,1,0:T(8,128)}), f32[16,256,128]{2,1,0:T(8,128)S(1)}, u32[]{:S(2)}, u32[]{:S(2)}) async-start(f32[16,256,128]{2,1,0:T(8,128)} %pack.6), calls=%async_computation.2 | async-start | bytes 4194304 | tf_op jit(solution)/shard_map/all_to_all | solution.py:342
  54.3 10.3 %advantage.1 = (f32[32,64,512]{2,1,0:T(8,128)}, f32[8,128]{1,0:T(8,128)}) custom-call(s32[1]{0:T(128)} %bitcast.4.here_ref, f32[32,64,512]{2,1,0:T(8,128)} %bitcast.17, f32[32,64,512]{2,1,0:T(8,128)} %bitcast.14, s32[5,512]{1,0:T(8,128)S(1)} %pad_add_fusion.times_ref, f32[2,512]{1,0:T(2,128)S(1)} %pad_maximum_fusion.rates_ref, f32[1,512]{1,0:T(1,128)} %bitcast.25, ...), custom_call_target="tpu_custom_call" | custom-call | flops 25165824 | bytes 12582912 | tf_op jit(solution)/shard_map/advantage/pallas_call | solution.py:240
  64.6 4.1 %pack.9 = f32[16,264,128]{2,1,0:T(8,128)} custom-call(f32[2048,512]{1,0:T(8,128)} %bitcast.20, f32[8,128]{1,0:T(8,128)} %get-tuple-element.65.refs_1_), custom_call_target="tpu_custom_call" | custom-call | bytes 4194304 | tf_op jit(solution)/shard_map/pack/pallas_call | solution.py:63
  68.7 4.7 %all-to-all-done.2.refs_0_ = f32[16,256,128]{2,1,0:T(8,128)S(1)} async-done(((f32[16,256,128]{2,1,0:T(8,128)}), f32[16,256,128]{2,1,0:T(8,128)S(1)}, u32[]{:S(2)}, u32[]{:S(2)}) %all-to-all-start.2) | async-done | bytes 2097184 | tf_op jit(solution)/shard_map/all_to_all | solution.py:342
  74.7 5.9 %all-to-all-start.3 = ((f32[16,264,128]{2,1,0:T(8,128)}), f32[16,264,128]{2,1,0:T(8,128)S(1)}, u32[]{:S(2)}, u32[]{:S(2)}) async-start(f32[16,264,128]{2,1,0:T(8,128)} %pack.9), calls=%async_computation.3 | async-start | bytes 4325376 | tf_op jit(solution)/shard_map/all_to_all | solution.py:342
  80.5 4.2 %pack.8 = f32[16,256,128]{2,1,0:T(8,128)} custom-call(f32[2048,512]{1,0:T(8,128)} %bitcast.21), custom_call_target="tpu_custom_call" | custom-call | bytes 4194304 | tf_op jit(solution)/shard_map/pack/pallas_call | solution.py:63
  84.7 15.5 %all-to-all-done.3.adv = f32[16,264,128]{2,1,0:T(8,128)S(1)} async-done(((f32[16,264,128]{2,1,0:T(8,128)}), f32[16,264,128]{2,1,0:T(8,128)S(1)}, u32[]{:S(2)}, u32[]{:S(2)}) %all-to-all-start.3) | async-done | bytes 2162720 | tf_op jit(solution)/shard_map/all_to_all | solution.py:342
  100.2 6.3 %all-to-all-start.4 = ((f32[16,256,128]{2,1,0:T(8,128)}), f32[16,256,128]{2,1,0:T(8,128)}, u32[]{:S(2)}, u32[]{:S(2)}) async-start(f32[16,256,128]{2,1,0:T(8,128)} %pack.8), calls=%async_computation.4 | async-start | bytes 4194304 | tf_op jit(solution)/shard_map/all_to_all | solution.py:342
  108.1 1.5 %collective-permute-start.1 = (f32[4]{0:T(128)S(1)}, f32[4]{0:T(128)S(1)}, u32[]{:S(2)}, u32[]{:S(2)}) collective-permute-start(f32[4]{0:T(128)S(1)} %pad_maximum_fusion.2), channel_id=1, source_target_pairs={{0,2},{2,4},{4,6},{6,0},{1,3},{3,5},{5,7},{7,1},{8,10},{10,12},{12... | collective-permute-start | bytes 56 | tf_op jit(solution)/shard_map/ppermute | solution.py:347
  109.6 3.3 %collective-permute-done.1 = f32[4]{0:T(128)S(1)} collective-permute-done((f32[4]{0:T(128)S(1)}, f32[4]{0:T(128)S(1)}, u32[]{:S(2)}, u32[]{:S(2)}) %collective-permute-start.1) | collective-permute-done | bytes 48 | tf_op jit(solution)/shard_map/ppermute | solution.py:347
  113.0 1.8 %collective-permute-start.2 = (f32[4]{0:T(128)S(1)}, f32[4]{0:T(128)S(1)}, u32[]{:S(2)}, u32[]{:S(2)}) collective-permute-start(f32[4]{0:T(128)S(1)} %pad_maximum_fusion.3), channel_id=1, source_target_pairs={{0,4},{2,6},{4,0},{6,2},{1,5},{3,7},{5,1},{7,3},{8,12},{10,14},{12... | collective-permute-start | bytes 56 | tf_op jit(solution)/shard_map/ppermute | solution.py:347
  114.8 3.2 %collective-permute-done.2 = f32[4]{0:T(128)S(1)} collective-permute-done((f32[4]{0:T(128)S(1)}, f32[4]{0:T(128)S(1)}, u32[]{:S(2)}, u32[]{:S(2)}) %collective-permute-start.2) | collective-permute-done | bytes 48 | tf_op jit(solution)/shard_map/ppermute | solution.py:347
  118.7 3.1 %pad_maximum_fusion.4.stat_ref = f32[4]{0:T(128)} fusion(f32[1]{0:T(128)} %get-tuple-element.86, f32[1]{0:T(128)} %get-tuple-element.83, f32[1]{0:T(128)} %get-tuple-element.87, f32[1]{0:T(128)} %get-tuple-element.82), kind=kLoop, calls=%fused_computation.24 | loop fusion | flops 12 | bytes 32 | tf_op jit(solution)/shard_map/stack | solution.py:403
  121.9 5.3 %normalized.2 = (f32[32,32768]{1,0:T(8,128)}, f32[32,32768]{1,0:T(8,128)}) custom-call(f32[4]{0:T(128)} %pad_maximum_fusion.4.stat_ref, f32[16,264,128]{2,1,0:T(8,128)} %copy-done, f32[16,128,128]{2,1,0:T(8,128)} %copy-done.3, f32[16,144,128]{2,1,0:T(8,128)} %copy-done.2), custom_call_target="tpu_custom_call" | custom-call | flops 2097152 | bytes 8388608 | tf_op jit(solution)/shard_map/normalized/pallas_call | solution.py:319
  127.2 5.1 %normalized.3 = (f32[32,32768]{1,0:T(8,128)}, f32[32,32768]{1,0:T(8,128)}) custom-call(f32[4]{0:T(128)} %pad_maximum_fusion.4.stat_ref, f32[16,256,128]{2,1,0:T(8,128)} %all-to-all-done.4.adv, f32[16,256,128]{2,1,0:T(8,128)} %copy-done.1, f32[32,32768]{1,0:T(8,128)} %get-tuple-element.72.refs_1_, ...), custom_call_target="tpu_custom_call", output_to_operand_aliasing={{0}: (3, {}), {1}: (4, {})} | custom-call | flops 2097152 | bytes 8388608 | tf_op jit(solution)/shard_map/normalized/pallas_call | solution.py:319
  (30 shorter events, 6.5 us)
Async XLA Ops:
  11.4 21.1 %all-to-all-start = ((f32[16,128,128]{2,1,0:T(8,128)}), f32[16,128,128]{2,1,0:T(8,128)S(1)}, u32[]{:S(2)}, u32[]{:S(2)}) async-start(f32[16,128,128]{2,1,0:T(8,128)} %pack.5), calls=%async_computation | async-start | bytes 2097152 | tf_op jit(solution)/shard_map/all_to_all | solution.py:342
  32.5 7.9 %copy-start.3 = (f32[16,128,128]{2,1,0:T(8,128)}, f32[16,128,128]{2,1,0:T(8,128)S(1)}, u32[]{:S(2)}) copy-start(f32[16,128,128]{2,1,0:T(8,128)S(1)} %all-to-all-done.refs_0_) | copy-start | bytes 3145732
  32.5 17.4 %all-to-all-start.1 = ((f32[16,144,128]{2,1,0:T(8,128)}), f32[16,144,128]{2,1,0:T(8,128)S(1)}, u32[]{:S(2)}, u32[]{:S(2)}) async-start(f32[16,144,128]{2,1,0:T(8,128)} %pack.7), calls=%async_computation.1 | async-start | bytes 2359296 | tf_op jit(solution)/shard_map/all_to_all | solution.py:342
  49.9 4.4 %copy-start.2 = (f32[16,144,128]{2,1,0:T(8,128)}, f32[16,144,128]{2,1,0:T(8,128)S(1)}, u32[]{:S(2)}) copy-start(f32[16,144,128]{2,1,0:T(8,128)S(1)} %all-to-all-done.1.refs_1_) | copy-start | bytes 3538948
  49.9 23.5 %all-to-all-start.2 = ((f32[16,256,128]{2,1,0:T(8,128)}), f32[16,256,128]{2,1,0:T(8,128)S(1)}, u32[]{:S(2)}, u32[]{:S(2)}) async-start(f32[16,256,128]{2,1,0:T(8,128)} %pack.6), calls=%async_computation.2 | async-start | bytes 4194304 | tf_op jit(solution)/shard_map/all_to_all | solution.py:342
  73.4 1.3 copy-start.1
  74.7 25.5 %all-to-all-start.3 = ((f32[16,264,128]{2,1,0:T(8,128)}), f32[16,264,128]{2,1,0:T(8,128)S(1)}, u32[]{:S(2)}, u32[]{:S(2)}) async-start(f32[16,264,128]{2,1,0:T(8,128)} %pack.9), calls=%async_computation.3 | async-start | bytes 4325376 | tf_op jit(solution)/shard_map/all_to_all | solution.py:342
  100.2 6.6 %copy-start = (f32[16,264,128]{2,1,0:T(8,128)}, f32[16,264,128]{2,1,0:T(8,128)S(1)}, u32[]{:S(2)}) copy-start(f32[16,264,128]{2,1,0:T(8,128)S(1)} %all-to-all-done.3.adv) | copy-start | bytes 6488068
  100.2 27.0 %all-to-all-start.4 = ((f32[16,256,128]{2,1,0:T(8,128)}), f32[16,256,128]{2,1,0:T(8,128)}, u32[]{:S(2)}, u32[]{:S(2)}) async-start(f32[16,256,128]{2,1,0:T(8,128)} %pack.8), calls=%async_computation.4 | async-start | bytes 4194304 | tf_op jit(solution)/shard_map/all_to_all | solution.py:342
  106.8 1.1 collective-permute-start
  108.1 4.8 %collective-permute-start.1 = (f32[4]{0:T(128)S(1)}, f32[4]{0:T(128)S(1)}, u32[]{:S(2)}, u32[]{:S(2)}) collective-permute-start(f32[4]{0:T(128)S(1)} %pad_maximum_fusion.2), channel_id=1, source_target_pairs={{0,2},{2,4},{4,6},{6,0},{1,3},{3,5},{5,7},{7,1},{8,10},{10,12},{12... | collective-permute-start | bytes 56 | tf_op jit(solution)/shard_map/ppermute | solution.py:347
  113.0 5.1 %collective-permute-start.2 = (f32[4]{0:T(128)S(1)}, f32[4]{0:T(128)S(1)}, u32[]{:S(2)}, u32[]{:S(2)}) collective-permute-start(f32[4]{0:T(128)S(1)} %pad_maximum_fusion.3), channel_id=1, source_target_pairs={{0,4},{2,6},{4,0},{6,2},{1,5},{3,7},{5,1},{7,3},{8,12},{10,14},{12... | collective-permute-start | bytes 56 | tf_op jit(solution)/shard_map/ppermute | solution.py:347

commit v3 on v2

--- a/solution.py
+++ b/solution.py
@@ -18,10 +18,11 @@
 ROWS = 256
 SMEM = pl.BlockSpec(memory_space=pltpu.SMEM)
 ANY = pl.BlockSpec(memory_space=pl.ANY)
-
-
-def params(**kw):
-    return pltpu.CompilerParams(vmem_limit_bytes=56 << 20, **kw)
+VMEM = pl.BlockSpec(memory_space=pltpu.VMEM)
+
+
+def params(mib=56):
+    return pltpu.CompilerParams(vmem_limit_bytes=mib << 20)
 
 
 def cost(flops, moved):
@@ -72,10 +73,15 @@
     )(block, *(() if rider is None else (rider,)))
 
 
-def stepper(times_ref, rates_ref, length):
+def stepper(here_ref, done_ref, taken_ref, discount_ref, retention_ref, length):
     first = lax.broadcasted_iota(jnp.int32, (SEG, LANES), 0) * length
-    marks = [times_ref[k : k + 1, :] for k in range(times_ref.shape[0])]
-    discount, retention = rates_ref[0:1, :], rates_ref[1:2, :]
+    start, horizon = here_ref[0], here_ref[1]
+    marks = [done_ref[k : k + 1, :] - start for k in range(done_ref.shape[0])]
+    full = horizon - 1 - taken_ref[...] - start
+    for _ in range(2):
+        full = jnp.where(full < 0, full + horizon, full)
+    marks.append(full)
+    discount, retention = discount_ref[...], retention_ref[...]
 
     def step(i, reward, value, next_value):
         time = first + i
@@ -98,9 +104,10 @@
     return jnp.concatenate([firsts[1:], boundary], axis=0)
 
 
-def summary_body(rew_ref, val_ref, times_ref, rates_ref, seg_ref, all_ref):
+def summary_body(here_ref, rew_ref, val_ref, *refs):
+    seg_ref, all_ref = refs[-2:]
     length = rew_ref.shape[1]
-    step = stepper(times_ref, rates_ref, length)
+    step = stepper(here_ref, *refs[:4], length)
     zero = jnp.zeros((SEG, LANES), F32)
 
     def eight(at, partial, product, following, last):
@@ -145,14 +152,15 @@
     return block.reshape(SEG, steps // SEG, envs)
 
 
-def summary(rewards, values, times, rates):
+def summary(here, rewards, values, *rest):
     steps, envs = rewards.shape
     groups = envs // LANES
     return pl.pallas_call(
         summary_body,
         grid=(groups,),
         in_specs=[
-            columns(SEG, steps // SEG), columns(SEG, steps // SEG), columns(len(times)), columns(2),
+            SMEM, columns(SEG, steps // SEG), columns(SEG, steps // SEG),
+            *(columns(len(part)) for part in rest),
         ],
         out_specs=[columns(3, SEG), pl.BlockSpec((4 * groups, LANES), lambda j: (0, 0))],
         out_shape=[
@@ -162,16 +170,17 @@
         compiler_params=params(),
         cost_estimate=cost(16 * steps * envs, 8 * steps * envs),
         name="summary",
-    )(segmented(rewards), segmented(values), times, rates)
+    )(here, segmented(rewards), segmented(values), *rest)
 
 
 def advantage_body(
-    here_ref, rew_ref, val_ref, times_ref, rates_ref, last_ref, seg_ref, every_ref, adv_ref, stat_ref
+    here_ref, rew_ref, val_ref, done_ref, taken_ref, discount_ref, retention_ref,
+    last_ref, seg_ref, every_ref, adv_ref, stat_ref,
 ):
     length = rew_ref.shape[1]
     group = pl.program_id(0)
-    here = here_ref[0]
-    step = stepper(times_ref, rates_ref, length)
+    here = here_ref[2]
+    step = stepper(here_ref, done_ref, taken_ref, discount_ref, retention_ref, length)
 
     boundary = last_ref[...]
     incoming = jnp.zeros((1, LANES), F32)
@@ -235,14 +244,14 @@
     stat_ref[...] = line
 
 
-def advantage(here, rewards, values, times, rates, last_value, segments, every):
+def advantage(here, rewards, values, rest, last_value, segments, every):
     steps, envs = rewards.shape
     adv, stats = pl.pallas_call(
         advantage_body,
         grid=(envs // LANES,),
         in_specs=[
-            SMEM, columns(SEG, steps // SEG), columns(SEG, steps // SEG), columns(len(times)),
-            columns(2), columns(1), columns(3, SEG), pl.BlockSpec(every.shape, lambda j: (0, 0, 0)),
+            SMEM, columns(SEG, steps // SEG), columns(SEG, steps // SEG),
+            *(columns(len(part)) for part in rest), columns(1), columns(3, SEG), pl.BlockSpec(every.shape, lambda j: (0, 0, 0)),
         ],
         out_specs=[columns(SEG, steps // SEG), pl.BlockSpec((8, LANES), lambda j: (0, 0))],
         out_shape=[
@@ -252,28 +261,90 @@
         compiler_params=params(),
         cost_estimate=cost(24 * steps * envs, 12 * steps * envs),
         name="advantage",
-    )(here, segmented(rewards), segmented(values), times, rates, last_value, segments, every)
+    )(here, segmented(rewards), segmented(values), *rest, last_value, segments, every)
     return adv.reshape(steps, envs), stats
 
 
-def normal_body(counts, steps, offset, stat_ref, adv, *refs):
-    vals = refs[: len(counts)]
-    out_adv, out_ret, abuf, vbuf, oabuf, orbuf, in_sem, out_sem = refs[-8:]
-    blocks, rows, _ = abuf.shape
-    own = out_adv.shape[0]
-    width = rows // own * LANES
-
-    def fetches(s):
-        copies = [pltpu.make_async_copy(adv.at[s, pl.ds(0, rows)], abuf.at[s], in_sem.at[0, s])]
-        at = 0
-        for k, (val, count) in enumerate(zip(vals, counts)):
-            copies.append(
-                pltpu.make_async_copy(
-                    val.at[s, pl.ds(0, count)], vbuf.at[s, pl.ds(at, count)], in_sem.at[k + 1, s]
-                )
-            )
-            at += count
-        return copies
+def merged(states, count):
+    lane = lax.broadcasted_iota(jnp.int32, states[0].shape, 1)
+    mean = sum(states[1:], states[0]) / len(states)
+    gaps = [(state - mean) * (state - mean) for state in states]
+    gaps = pltpu.roll(sum(gaps[1:], gaps[0]), 2, 1)
+    square = sum(states[1:], states[0]) + count * gaps
+    return jnp.where(lane < 2, mean, jnp.where(lane < 4, square, 0.0))
+
+
+def gather_body(groups, count, part_ref, o_ref):
+    sums = part_ref[:, 0, :]
+    lane = lax.broadcasted_iota(jnp.int32, sums.shape, 1)
+    kind = lane % 4
+
+    def total(k, values):
+        return jnp.sum(jnp.where((kind == k) & (lane < 4 * groups), values, 0.0))
+
+    whole = count * groups * sums.shape[0]
+    means = [total(k, sums) / whole for k in range(2)]
+    off = sums / count - jnp.where(kind == 0, means[0], means[1])
+    off = count * off * off
+    squares = [total(k + 2, sums) + total(k, off) for k in range(2)]
+    lane = lax.broadcasted_iota(jnp.int32, o_ref.shape, 1)
+    line = jnp.zeros(o_ref.shape, F32)
+    for k, value in enumerate(means + squares):
+        line = jnp.where(lane == k, value, line)
+    o_ref[...] = line
+
+
+def gathered(adv, rows, groups, count):
+    blocks = adv.shape[0]
+    return pl.pallas_call(
+        functools.partial(gather_body, groups, float(count)),
+        grid=(1,),
+        in_specs=[pl.BlockSpec((blocks, 8, LANES), lambda i: (0, rows // 8, 0))],
+        out_specs=pl.BlockSpec((8, LANES), lambda i: (0, 0)),
+        out_shape=jax.ShapeDtypeStruct((8, LANES), F32),
+        compiler_params=params(16),
+        cost_estimate=cost(1000, 4096 * blocks),
+        name="gathered",
+    )(adv)
+
+
+def merge_body(count, *refs):
+    refs[-1][...] = merged([ref[...] for ref in refs[:-1]], count)
+
+
+def merge(states, count):
+    return pl.pallas_call(
+        functools.partial(merge_body, float(count)),
+        in_specs=[VMEM] * len(states),
+        out_specs=VMEM,
+        out_shape=jax.ShapeDtypeStruct(states[0].shape, F32),
+        compiler_params=params(16),
+        cost_estimate=cost(1000, 4096 * len(states)),
+        name="merge",
+    )(*states)
+
+
+def around(state, axis):
+    size = lax.axis_size(axis)
+    return [state] + [
+        lax.ppermute(state, axis, [(i, (i + far) % size) for i in range(size)])
+        for far in range(1, size)
+    ]
+
+
+def normal_body(parts, n_states, count, steps, offset, *refs):
+    states, adv = refs[:n_states], refs[n_states]
+    vals = refs[n_states + 1 : n_states + 1 + len(parts)]
+    out_adv, out_ret, oabuf, orbuf, out_sem = refs[-5:]
+    blocks, own, width = oabuf.shape
+
+    state = merged([ref[...] for ref in states], count)
+    scale = 1.0 / jnp.sqrt(state / (count * n_states) + 1e-05)
+    first = lax.broadcasted_iota(jnp.int32, state.shape, 0) == 0
+    lane = lax.broadcasted_iota(jnp.int32, state.shape, 1)
+    pick = lambda values, k: jnp.sum(jnp.where(first & (lane == k), values, 0.0))
+    mean_adv, mean_ret = pick(state, 0), pick(state, 1)
+    scale_adv, scale_ret = pick(scale, 2), pick(scale, 3)
 
     def stores(s):
         place = pl.ds(pl.multiple_of(s * steps + offset, LANES), width)
@@ -282,73 +353,55 @@
             for k, (buf, out) in enumerate(((oabuf, out_adv), (orbuf, out_ret)))
         ]
 
-    def each(body):
-        lax.fori_loop(0, blocks, lambda s, c: (body(s), c)[1], 0)
-
-    def begin(s):
-        for copy in fetches(s):
-            copy.start()
-
-    def work(s):
-        for copy in fetches(s):
-            copy.wait()
-        for h in range(rows // own):
-            part = abuf[s, h * own : (h + 1) * own, :]
-            ret = part + vbuf[s, h * own : (h + 1) * own, :]
-            lanes = slice(h * LANES, (h + 1) * LANES)
-            oabuf[s, :, lanes] = (part - stat_ref[0]) * stat_ref[1]
-            orbuf[s, :, lanes] = (ret - stat_ref[2]) * stat_ref[3]
+    def work(s, carry):
+        h = 0
+        for val, (begin, end) in zip(vals, parts):
+            for at in range(begin, end, own):
+                part = adv[s, h * own : (h + 1) * own, :]
+                ret = part + val[s, at : at + own, :]
+                lanes = slice(h * LANES, (h + 1) * LANES)
+                oabuf[s, :, lanes] = (part - mean_adv) * scale_adv
+                orbuf[s, :, lanes] = (ret - mean_ret) * scale_ret
+                h += 1
         for copy in stores(s):
             copy.start()
-
-    def finish(s):
+        return carry
+
+    def finish(s, carry):
         for copy in stores(s):
             copy.wait()
-
-    each(begin)
-    each(work)
-    each(finish)
-
-
-def normalized(stats, adv, vals, counts, own, steps, offset, into=None):
-    blocks, rows = adv.shape[0], sum(counts)
+        return carry
+
+    lax.fori_loop(0, blocks, work, 0)
+    lax.fori_loop(0, blocks, finish, 0)
+
+
+def normalized(states, count, adv, vals, parts, own, steps, offset, into=()):
+    blocks, rows = adv.shape[0], sum(end - begin for begin, end in parts)
     shape = jax.ShapeDtypeStruct((own, blocks * steps), F32)
-    into = () if into is None else tuple(into)
-    at = 2 + len(vals)
+    at = len(states) + 1 + len(vals)
     width = rows // own * LANES
     return pl.pallas_call(
-        functools.partial(normal_body, counts, steps, offset),
-        in_specs=[SMEM] + [ANY] * (1 + len(vals) + len(into)),
+        functools.partial(normal_body, parts, len(states), float(count), steps, offset),
+        in_specs=[VMEM] * at + [ANY] * len(into),
         out_specs=[ANY, ANY],
         out_shape=[shape, shape],
         input_output_aliases={at + k: k for k in range(len(into))},
         scratch_shapes=[
-            pltpu.VMEM((blocks, rows, LANES), F32),
-            pltpu.VMEM((blocks, rows, LANES), F32),
             pltpu.VMEM((blocks, own, width), F32),
             pltpu.VMEM((blocks, own, width), F32),
-            pltpu.SemaphoreType.DMA((1 + len(vals), blocks)),
             pltpu.SemaphoreType.DMA((2, blocks)),
         ],
-        compiler_params=params(),
+        compiler_params=params(20),
         cost_estimate=cost(4 * blocks * rows * LANES, 16 * blocks * rows * LANES),
         name="normalized",
-    )(stats, adv, *vals, *into)
+    )(*states, adv, *vals, *into)
 
 
 def exchange(packed, behind=None):
     if behind is not None:
         packed, behind = lax.optimization_barrier((packed, behind))
     return lax.all_to_all(packed, TM, 0, 0, tiled=True), behind
-
-
-def merged(mean, square, count, axis, distance):
-    size = lax.axis_size(axis)
-    other = lax.ppermute(
-        jnp.concatenate([mean, square]), axis, [(i, (i + distance) % size) for i in range(size)]
-    )
-    gap = other[:2] - mean
-    return mean + 0.5 * gap, square + other[2:] + (0.5 * count) * gap * gap, 2.0 * count
 
 
 def shards(rewards, values, last_value, done_steps, horizon_offset, discount_rate, trace_rate):
@@ -358,53 +411,54 @@
     horizon = steps * blocks // 2
     groups = envs // LANES
     own = envs // blocks
-    half, quarter = steps // 2, steps // 4
+    one, two, cut = 512, 512, 1024
     rows = lambda count: count // LANES * own
 
     discount = jnp.exp(-discount_rate)
-    rates = jnp.stack([discount, discount * jnp.exp(-trace_rate)])
-    truncated = jnp.mod(horizon - 1 - horizon_offset - here * steps, horizon)
-    times = jnp.concatenate([done_steps.T - here * steps, truncated[None]], axis=0)
+    retention = discount * jnp.exp(-trace_rate)
+    rest = (done_steps.T, horizon_offset[None], discount[None], retention[None])
+    where = jnp.stack([here * steps, jnp.int32(horizon), here])
 
     core = lax.axis_index(ENV[1])
-    given = (rewards, values, times, rates)
+    given = (where, rewards, values, *rest)
     blank = lambda *_: (
         jnp.zeros((3, SEG, envs), F32),
         jnp.zeros((4 * groups, LANES), F32),
     )
     ahead = lax.cond(core == 0, lambda *x: tuple(summary(*x)), blank, *given)
     values_1, ahead = lax.optimization_barrier((values, ahead))
-    packed, ahead = lax.optimization_barrier((pack(values_1, blocks, 0, quarter), ahead))
+    packed, ahead = lax.optimization_barrier((pack(values_1, blocks, 0, one), ahead))
     val_1, _ = exchange(packed)
     segments, whole = lax.cond(
         core == 0, lambda done, *_: done, lambda _, *x: tuple(summary(*x)), ahead, *given
     )
 
-    val_2, val_1 = exchange(pack(values, blocks, quarter, quarter, whole), val_1)
-    val_3, val_2 = exchange(pack(values, blocks, half, half), val_2)
-    every = val_2[:, rows(quarter) :, :]
+    val_2, val_1 = exchange(pack(values, blocks, one, two, whole), val_1)
+    val_3, val_2 = exchange(pack(values, blocks, one + two, steps - one - two), val_2)
+    every = val_2[:, rows(two) :, :]
     adv, local = advantage(
-        here.reshape(1), rewards, values, times, rates, last_value[None], segments, every
-    )
-    adv_1, val_3 = exchange(pack(adv, blocks, 0, half, local), val_3)
-    adv_2, adv_1 = exchange(pack(adv, blocks, half, half), adv_1)
-
-    parts = adv_1[:, rows(half), : 4 * groups].reshape(-1, 4)
-    count = float(steps * LANES)
-    means = parts[:, :2] / count
-    mean = jnp.mean(means, axis=0)
-    off = means - mean
-    square = jnp.sum(parts[:, 2:] + count * off * off, axis=0)
+        where, rewards, values, rest, last_value[None], segments, every
+    )
+    adv_1, val_3 = exchange(pack(adv, blocks, 0, cut, local), val_3)
+    adv_2, adv_1 = exchange(pack(adv, blocks, cut, steps - cut), adv_1)
+
+    count = steps * LANES
+    state = gathered(adv_1, rows(cut), groups, count)
     count = count * groups * blocks
-    mean, square, count = merged(mean, square, count, ENV[1], 1)
-    mean, square, count = merged(mean, square, count, ENV[0], 1)
-    mean, square, count = merged(mean, square, count, ENV[0], 2)
-    scale = 1.0 / jnp.sqrt(square / count + 1e-05)
-    stats = jnp.stack([mean[0], scale[0], mean[1], scale[1]])
-
-    counts = (rows(quarter), rows(quarter))
-    out = normalized(stats, adv_1, (val_1, val_2), counts, own, steps, 0)
-    return tuple(normalized(stats, adv_2, (val_3,), (rows(half),), own, steps, half, out))
+    state = merge(around(state, ENV[0]), count)
+    count = count * lax.axis_size(ENV[0])
+    states = around(state, ENV[1])
+
+    held = ((val_1, 0, one), (val_2, one, one + two), (val_3, one + two, steps))
+
+    def write(adv, begin, end, into=()):
+        taken = [(val, max(lo, begin) - lo, min(hi, end) - lo) for val, lo, hi in held]
+        taken = [part for part in taken if part[1] < part[2]]
+        vals = tuple(val for val, _, _ in taken)
+        parts = tuple((rows(lo), rows(hi)) for _, lo, hi in taken)
+        return normalized(states, count, adv, vals, parts, own, steps, begin, into)
+
+    return tuple(write(adv_2, cut, steps, write(adv_1, 0, cut)))
 
 
 def solution(mesh):

time: 133 us -> 130 us (0.977)
  other arithmetic: 5.85 us -> 0.78 us
  waiting for transfers between devices: 47.7 us -> 51.4 us
  Pallas kernels: 44.1 us -> 40.7 us
    all_to_all x5, waiting for transfers between devices: 40.1 us -> 46.3 us  [exchange(): return (lax.all_to_all(packed, TM, 0, 0, tiled=True), behind)]
    pallas_call x3 -> x5, Pallas kernels: 16.7 us -> 13.3 us  [the longest x2 6.56 us: normalized(): pl.pallas_call(functools.partial(normal_body, parts, len(states), float(c...]
    another operation x2 -> x1, other arithmetic: 3.15 us -> 0.08 us  [shards(): where = jnp.stack([here * steps, jnp.int32(horizon), here])]
    ppermute x3 -> x4, waiting for transfers between devices: 7.6 us -> 5.08 us  [around(): lax.ppermute(state, axis, [(i, (i + far) % size) for i in range(size)])]
    unnamed x8 -> x12, local copies, waits for them, and re-layouts: 1.31 us -> 2.94 us
    ppermute x3 -> x4, starting transfers between devices: 3.34 us -> 4.53 us  [around(): lax.ppermute(state, axis, [(i, (i + far) % size) for i in range(size)])]
  transfers between devices with their start and end apart: 8 -> 9, of which waited for: 7 -> 8; matrix products, arithmetic and copies ran while one was open for 4% -> 1% of each run, Pallas kernels for 23% -> 22%
where the time goes in v3:
time: 130 us; the launch traced here: 129 us
  waiting for transfers between devices  51.4 us (40%)
  Pallas kernels  40.7 us (31%)
  starting transfers between devices  32.2 us (25%)
  local copies, waits for them, and re-layouts  3.61 us (3%)
    all_to_all x5, waiting for transfers between devices, exchange(): return (lax.all_to_all(packed, TM, 0, 0, tiled=True), behind)  46.3 us
    all_to_all x5, starting transfers between devices, exchange(): return (lax.all_to_all(packed, TM, 0, 0, tiled=True), behind)  27.7 us
    pallas_call x5, Pallas kernels, pack(): pl.pallas_call(functools.partial(pack_body, dests, riders), grid=(count /...  17.1 us
    pallas_call x1, Pallas kernels, advantage(): pl.pallas_call(advantage_body, grid=(envs // LANES,), in_specs=[SMEM, col...  10.3 us
    pallas_call x2, Pallas kernels, normalized(): pl.pallas_call(functools.partial(normal_body, parts, len(states), float(c...  6.56 us
    pallas_call x1, Pallas kernels, summary(): pl.pallas_call(summary_body, grid=(groups,), in_specs=[SMEM, columns(SEG,...  6.39 us
    ppermute x4, waiting for transfers between devices, around(): lax.ppermute(state, axis, [(i, (i + far) % size) for i in range(size)])  5.08 us
    ppermute x4, starting transfers between devices, around(): lax.ppermute(state, axis, [(i, (i + far) % size) for i in range(size)])  4.53 us
  transfers between devices with their start and end apart: 9, of which 8 were waited for; matrix products, arithmetic and copies ran while one was open for 1% of the time, Pallas kernels for 22%

profile of v3, /device:TPU:0, one launch (start us, length us, event | category | flops | bytes accessed | tf_op | source)
XLA Modules:
  0.0 129.5 jit_solution(10012059078176921099)
XLA Ops:
  1.4 6.4 %conditional.2 = ((f32[3,32,512]{2,1,0:T(8,128)S(1)}, f32[16,128]{1,0:T(8,128)S(1)})) conditional(s32[]{:T(128)} %convert_element_type.4, () %tuple.27, (f32[2048,512]{1,0:T(8,128)}, f32[2048,512]{1,0:T(8,128)}, s32[3]{0:T(128)S(1)}, s32[4,512]{1,0:T(4,128)}, s32[1,512]{1,0:T(1,128)}, /*index=5*/f32[1,512]{1,0:T(1,128)S(1)}, ...), branch_computations={%region_0.0_spmd, %region_1.0_spmd} | conditional | flops 16777216 | bytes 8388616 | solution.py:428
  1.4 6.4 %summary.2 = (f32[3,32,512]{2,1,0:T(8,128)S(1)}, f32[16,128]{1,0:T(8,128)S(1)}) custom-call(s32[3]{0:T(128)S(1)} %get-tuple-element.32.here_ref, f32[32,64,512]{2,1,0:T(8,128)} %bitcast.18, f32[32,64,512]{2,1,0:T(8,128)} %bitcast.15, s32[4,512]{1,0:T(4,128)} %get-tuple-element.35.refs_0_, s32[1,512]{1,0:T(1,128)} %get-tuple-element.36.refs_1_, ...), custom_call_target="tpu_custom_call" | custom-call | flops 16777216 | bytes 8388608 | tf_op jit(solution)/shard_map/cond/branch_1_fun/summary/pallas_call | solution.py:158
  7.8 2.3 %pack.5 = f32[16,128,128]{2,1,0:T(8,128)} custom-call(f32[2048,512]{1,0:T(8,128)} %refs_0_.4), custom_call_target="tpu_custom_call" | custom-call | bytes 2097152 | tf_op jit(solution)/shard_map/pack/pallas_call | solution.py:64
  10.1 8.1 %all-to-all-start = ((f32[16,128,128]{2,1,0:T(8,128)}), f32[16,128,128]{2,1,0:T(8,128)S(1)}, u32[]{:S(2)}, u32[]{:S(2)}) async-start(f32[16,128,128]{2,1,0:T(8,128)} %pack.5), calls=%async_computation | async-start | bytes 2097152 | tf_op jit(solution)/shard_map/all_to_all | solution.py:404
  18.3 2.5 %pack.7 = f32[16,144,128]{2,1,0:T(8,128)} custom-call(f32[2048,512]{1,0:T(8,128)} %refs_0_.4, f32[16,128]{1,0:T(8,128)S(1)} %get-tuple-element.78.refs_1_), custom_call_target="tpu_custom_call" | custom-call | bytes 2097152 | tf_op jit(solution)/shard_map/pack/pallas_call | solution.py:64
  20.8 10.4 %all-to-all-done.refs_3_ = f32[16,128,128]{2,1,0:T(8,128)S(1)} async-done(((f32[16,128,128]{2,1,0:T(8,128)}), f32[16,128,128]{2,1,0:T(8,128)S(1)}, u32[]{:S(2)}, u32[]{:S(2)}) %all-to-all-start) | async-done | bytes 1048608 | tf_op jit(solution)/shard_map/all_to_all | solution.py:404
  31.2 3.7 %all-to-all-start.1 = ((f32[16,144,128]{2,1,0:T(8,128)}), f32[16,144,128]{2,1,0:T(8,128)S(1)}, u32[]{:S(2)}, u32[]{:S(2)}) async-start(f32[16,144,128]{2,1,0:T(8,128)} %pack.7), calls=%async_computation.1 | async-start | bytes 2359296 | tf_op jit(solution)/shard_map/all_to_all | solution.py:404
  34.9 4.1 %pack.6 = f32[16,256,128]{2,1,0:T(8,128)} custom-call(f32[2048,512]{1,0:T(8,128)} %refs_0_.4), custom_call_target="tpu_custom_call" | custom-call | bytes 4194304 | tf_op jit(solution)/shard_map/pack/pallas_call | solution.py:64
  39.0 9.6 %all-to-all-done.1.refs_4_ = f32[16,144,128]{2,1,0:T(8,128)S(1)} async-done(((f32[16,144,128]{2,1,0:T(8,128)}), f32[16,144,128]{2,1,0:T(8,128)S(1)}, u32[]{:S(2)}, u32[]{:S(2)}) %all-to-all-start.1) | async-done | bytes 1179680 | tf_op jit(solution)/shard_map/all_to_all | solution.py:404
  48.6 3.7 %all-to-all-start.2 = ((f32[16,256,128]{2,1,0:T(8,128)}), f32[16,256,128]{2,1,0:T(8,128)S(1)}, u32[]{:S(2)}, u32[]{:S(2)}) async-start(f32[16,256,128]{2,1,0:T(8,128)} %pack.6), calls=%async_computation.2 | async-start | bytes 4194304 | tf_op jit(solution)/shard_map/all_to_all | solution.py:404
  53.0 10.3 %advantage.1 = (f32[32,64,512]{2,1,0:T(8,128)}, f32[8,128]{1,0:T(8,128)}) custom-call(s32[3]{0:T(128)S(1)} %pad_add_fusion.here_ref, f32[32,64,512]{2,1,0:T(8,128)} %bitcast.17, f32[32,64,512]{2,1,0:T(8,128)} %bitcast.14, s32[4,512]{1,0:T(4,128)S(1)} %bitcast.24, s32[1,512]{1,0:T(1,128)S(1)} %bitcast.33, f32[1,512]{1,0:T(1,128)S(1)} %bitcast.30, ...), custom_call_target="tpu_custom_call" | custom-call | flops 25165824 | bytes 12582912 | tf_op jit(solution)/shard_map/advantage/pallas_call | solution.py:249
  63.3 4.1 %pack.9 = f32[16,264,128]{2,1,0:T(8,128)} custom-call(f32[2048,512]{1,0:T(8,128)} %bitcast.20, f32[8,128]{1,0:T(8,128)} %get-tuple-element.83.refs_1_), custom_call_target="tpu_custom_call" | custom-call | bytes 4194304 | tf_op jit(solution)/shard_map/pack/pallas_call | solution.py:64
  67.4 4.6 %all-to-all-done.2.refs_3_ = f32[16,256,128]{2,1,0:T(8,128)S(1)} async-done(((f32[16,256,128]{2,1,0:T(8,128)}), f32[16,256,128]{2,1,0:T(8,128)S(1)}, u32[]{:S(2)}, u32[]{:S(2)}) %all-to-all-start.2) | async-done | bytes 2097184 | tf_op jit(solution)/shard_map/all_to_all | solution.py:404
  72.0 1.3 %copy-done = f32[16,256,128]{2,1,0:T(8,128)} copy-done((f32[16,256,128]{2,1,0:T(8,128)}, f32[16,256,128]{2,1,0:T(8,128)S(1)}, u32[]{:S(2)}) %copy-start) | copy-done | bytes 2097176
  73.4 5.8 %all-to-all-start.3 = ((f32[16,264,128]{2,1,0:T(8,128)}), f32[16,264,128]{2,1,0:T(8,128)S(1)}, u32[]{:S(2)}, u32[]{:S(2)}) async-start(f32[16,264,128]{2,1,0:T(8,128)} %pack.9), calls=%async_computation.3 | async-start | bytes 4325376 | tf_op jit(solution)/shard_map/all_to_all | solution.py:404
  79.2 4.1 %pack.8 = f32[16,256,128]{2,1,0:T(8,128)} custom-call(f32[2048,512]{1,0:T(8,128)} %bitcast.21), custom_call_target="tpu_custom_call" | custom-call | bytes 4194304 | tf_op jit(solution)/shard_map/pack/pallas_call | solution.py:64
  83.4 15.5 %all-to-all-done.3.part_ref.refs_2_ = f32[16,264,128]{2,1,0:T(8,128)S(1)} async-done(((f32[16,264,128]{2,1,0:T(8,128)}), f32[16,264,128]{2,1,0:T(8,128)S(1)}, u32[]{:S(2)}, u32[]{:S(2)}) %all-to-all-start.3) | async-done | bytes 2162720 | tf_op jit(solution)/shard_map/all_to_all | solution.py:404
  98.8 6.3 %all-to-all-start.4 = ((f32[16,256,128]{2,1,0:T(8,128)}), f32[16,256,128]{2,1,0:T(8,128)}, u32[]{:S(2)}, u32[]{:S(2)}) async-start(f32[16,256,128]{2,1,0:T(8,128)} %pack.8), calls=%async_computation.4 | async-start | bytes 4194304 | tf_op jit(solution)/shard_map/all_to_all | solution.py:404
  105.4 2.8 %collective-permute-start.2 = (f32[8,128]{1,0:T(8,128)S(1)}, f32[8,128]{1,0:T(8,128)S(1)}, u32[]{:S(2)}, u32[]{:S(2)}) collective-permute-start(f32[8,128]{1,0:T(8,128)S(1)} %gathered.1.refs_0_), channel_id=1, source_target_pairs={{0,6},{2,0},{4,2},{6,4},{1,7},{3,1},{5,3},{7,5},{8,14},{10,8},{12,... | collective-permute-start | bytes 12296 | tf_op jit(solution)/shard_map/ppermute | solution.py:330
  110.0 3.4 %collective-permute-done.1.refs_2_ = f32[8,128]{1,0:T(8,128)S(1)} collective-permute-done((f32[8,128]{1,0:T(8,128)S(1)}, f32[8,128]{1,0:T(8,128)S(1)}, u32[]{:S(2)}, u32[]{:S(2)}) %collective-permute-start.1) | collective-permute-done | bytes 4128 | tf_op jit(solution)/shard_map/ppermute | solution.py:330
  115.1 2.5 %normalized.2 = (f32[32,32768]{1,0:T(8,128)}, f32[32,32768]{1,0:T(8,128)}) custom-call(f32[8,128]{1,0:T(8,128)S(1)} %merge.1.refs_0_, f32[8,128]{1,0:T(8,128)S(1)} %collective-permute-done.3.refs_1_, f32[16,264,128]{2,1,0:T(8,128)S(1)} %all-to-all-done.3.part_ref.refs_2_, f32[16,128,128]{2,1,0:T(8,128)S(1)} %copy-done.3, ...), custom_call_target="tpu_custom_call" | custom-call | flops 2097152 | bytes 8388608 | tf_op jit(solution)/shard_map/normalized/pallas_call | solution.py:384
  117.6 6.1 %all-to-all-done.4.refs_2_ = f32[16,256,128]{2,1,0:T(8,128)} async-done(((f32[16,256,128]{2,1,0:T(8,128)}), f32[16,256,128]{2,1,0:T(8,128)}, u32[]{:S(2)}, u32[]{:S(2)}) %all-to-all-start.4) | async-done | bytes 2097184 | tf_op jit(solution)/shard_map/all_to_all | solution.py:404
  123.8 1.6 %copy-done.1 = f32[16,256,128]{2,1,0:T(8,128)S(1)} copy-done((f32[16,256,128]{2,1,0:T(8,128)S(1)}, f32[16,256,128]{2,1,0:T(8,128)}, u32[]{:S(2)}) %copy-start.1) | copy-done | bytes 2097176
  125.4 4.1 %normalized.3 = (f32[32,32768]{1,0:T(8,128)}, f32[32,32768]{1,0:T(8,128)}) custom-call(f32[8,128]{1,0:T(8,128)S(1)} %merge.1.refs_0_, f32[8,128]{1,0:T(8,128)S(1)} %collective-permute-done.3.refs_1_, f32[16,256,128]{2,1,0:T(8,128)} %all-to-all-done.4.refs_2_, f32[16,256,128]{2,1,0:T(8,128)S(1)} %copy-done.1, ...), custom_call_target="tpu_custom_call", output_to_operand_aliasing={{0}: (4, {}), {1}: (5, {})} | custom-call | flops 2097152 | bytes 8388608 | tf_op jit(solution)/shard_map/normalized/pallas_call | solution.py:384
  (22 shorter events, 5.2 us)
Async XLA Ops:
  7.8 2.3 %copy-start.4 = (s32[512,4]{0,1:T(4,128)S(1)}, s32[512,4]{0,1:T(4,128)}, u32[]{:S(2)}) copy-start(s32[512,4]{0,1:T(4,128)} %param.14) | copy-start | bytes 24580
  7.8 2.3 %copy-start.5 = (s32[512]{0:T(512)S(1)}, s32[512]{0:T(512)}, u32[]{:S(2)}) copy-start(s32[512]{0:T(512)} %param.15) | copy-start | bytes 6148
  10.1 21.1 %all-to-all-start = ((f32[16,128,128]{2,1,0:T(8,128)}), f32[16,128,128]{2,1,0:T(8,128)S(1)}, u32[]{:S(2)}, u32[]{:S(2)}) async-start(f32[16,128,128]{2,1,0:T(8,128)} %pack.5), calls=%async_computation | async-start | bytes 2097152 | tf_op jit(solution)/shard_map/all_to_all | solution.py:404
  31.2 7.8 %copy-start.2 = (f32[16,128,128]{2,1,0:T(8,128)}, f32[16,128,128]{2,1,0:T(8,128)S(1)}, u32[]{:S(2)}) copy-start(f32[16,128,128]{2,1,0:T(8,128)S(1)} %all-to-all-done.refs_3_) | copy-start | bytes 3145732
  31.2 17.4 %all-to-all-start.1 = ((f32[16,144,128]{2,1,0:T(8,128)}), f32[16,144,128]{2,1,0:T(8,128)S(1)}, u32[]{:S(2)}, u32[]{:S(2)}) async-start(f32[16,144,128]{2,1,0:T(8,128)} %pack.7), calls=%async_computation.1 | async-start | bytes 2359296 | tf_op jit(solution)/shard_map/all_to_all | solution.py:404
  48.6 23.4 %all-to-all-start.2 = ((f32[16,256,128]{2,1,0:T(8,128)}), f32[16,256,128]{2,1,0:T(8,128)S(1)}, u32[]{:S(2)}, u32[]{:S(2)}) async-start(f32[16,256,128]{2,1,0:T(8,128)} %pack.6), calls=%async_computation.2 | async-start | bytes 4194304 | tf_op jit(solution)/shard_map/all_to_all | solution.py:404
  72.0 1.3 %copy-start = (f32[16,256,128]{2,1,0:T(8,128)}, f32[16,256,128]{2,1,0:T(8,128)S(1)}, u32[]{:S(2)}) copy-start(f32[16,256,128]{2,1,0:T(8,128)S(1)} %all-to-all-done.2.refs_3_) | copy-start | bytes 6291460
  73.4 25.5 %all-to-all-start.3 = ((f32[16,264,128]{2,1,0:T(8,128)}), f32[16,264,128]{2,1,0:T(8,128)S(1)}, u32[]{:S(2)}, u32[]{:S(2)}) async-start(f32[16,264,128]{2,1,0:T(8,128)} %pack.9), calls=%async_computation.3 | async-start | bytes 4325376 | tf_op jit(solution)/shard_map/all_to_all | solution.py:404
  98.8 24.9 %all-to-all-start.4 = ((f32[16,256,128]{2,1,0:T(8,128)}), f32[16,256,128]{2,1,0:T(8,128)}, u32[]{:S(2)}, u32[]{:S(2)}) async-start(f32[16,256,128]{2,1,0:T(8,128)} %pack.8), calls=%async_computation.4 | async-start | bytes 4194304 | tf_op jit(solution)/shard_map/all_to_all | solution.py:404
  105.2 10.0 %copy-start.3 = (f32[16,128,128]{2,1,0:T(8,128)S(1)}, f32[16,128,128]{2,1,0:T(8,128)}, u32[]{:S(2)}) copy-start(f32[16,128,128]{2,1,0:T(8,128)} %copy-done.2) | copy-start | bytes 3145732
  105.4 4.5 %collective-permute-start.2 = (f32[8,128]{1,0:T(8,128)S(1)}, f32[8,128]{1,0:T(8,128)S(1)}, u32[]{:S(2)}, u32[]{:S(2)}) collective-permute-start(f32[8,128]{1,0:T(8,128)S(1)} %gathered.1.refs_0_), channel_id=1, source_target_pairs={{0,6},{2,0},{4,2},{6,4},{1,7},{3,1},{5,3},{7,5},{8,14},{10,8},{12,... | collective-permute-start | bytes 12296 | tf_op jit(solution)/shard_map/ppermute | solution.py:330
  108.3 5.1 %collective-permute-start.1 = (f32[8,128]{1,0:T(8,128)S(1)}, f32[8,128]{1,0:T(8,128)S(1)}, u32[]{:S(2)}, u32[]{:S(2)}) collective-permute-start(f32[8,128]{1,0:T(8,128)S(1)} %gathered.1.refs_0_), channel_id=1, source_target_pairs={{0,4},{2,6},{4,0},{6,2},{1,5},{3,7},{5,1},{7,3},{8,12},{10,14},{12... | collective-permute-start | bytes 12296 | tf_op jit(solution)/shard_map/ppermute | solution.py:330
  109.1 4.8 %collective-permute-start = (f32[8,128]{1,0:T(8,128)S(1)}, f32[8,128]{1,0:T(8,128)S(1)}, u32[]{:S(2)}, u32[]{:S(2)}) collective-permute-start(f32[8,128]{1,0:T(8,128)S(1)} %gathered.1.refs_0_), channel_id=1, source_target_pairs={{0,2},{2,4},{4,6},{6,0},{1,3},{3,5},{5,7},{7,1},{8,10},{10,12},{12... | collective-permute-start | bytes 12296 | tf_op jit(solution)/shard_map/ppermute | solution.py:330
  114.0 1.2 collective-permute-start.3
  123.8 1.6 %copy-start.1 = (f32[16,256,128]{2,1,0:T(8,128)S(1)}, f32[16,256,128]{2,1,0:T(8,128)}, u32[]{:S(2)}) copy-start(f32[16,256,128]{2,1,0:T(8,128)} %copy-done) | copy-start | bytes 6291460

commit v4 on v3

--- a/solution.py
+++ b/solution.py
@@ -15,7 +15,7 @@
 F32 = jnp.float32
 LANES = 128
 SEG = 32
-ROWS = 256
+ROWS = 128
 SMEM = pl.BlockSpec(memory_space=pltpu.SMEM)
 ANY = pl.BlockSpec(memory_space=pl.ANY)
 VMEM = pl.BlockSpec(memory_space=pltpu.VMEM)

time: 130 us -> 135 us (1.038)
  Pallas kernels: 40.7 us -> 48.7 us
  waiting for transfers between devices: 51.4 us -> 46.6 us
    pallas_call x5, Pallas kernels: 17.1 us -> 25.1 us  [pack(): pl.pallas_call(functools.partial(pack_body, dests, riders), grid=(count /...]
    all_to_all x5, waiting for transfers between devices: 46.3 us -> 41.5 us  [exchange(): return (lax.all_to_all(packed, TM, 0, 0, tiled=True), behind)]
  transfers between devices with their start and end apart: 9 -> 9, of which waited for: 8 -> 8; matrix products, arithmetic and copies ran while one was open for 1% -> 0% of each run, Pallas kernels for 22% -> 26%
where the time goes in v4:
time: 135 us; the launch traced here: 134 us
  Pallas kernels  48.7 us (36%)
  waiting for transfers between devices  46.6 us (35%)
  starting transfers between devices  33.4 us (25%)
  local copies, waits for them, and re-layouts  3.61 us (3%)
    all_to_all x5, waiting for transfers between devices, exchange(): return (lax.all_to_all(packed, TM, 0, 0, tiled=True), behind)  41.5 us
    all_to_all x5, starting transfers between devices, exchange(): return (lax.all_to_all(packed, TM, 0, 0, tiled=True), behind)  28.9 us
    pallas_call x5, Pallas kernels, pack(): pl.pallas_call(functools.partial(pack_body, dests, riders), grid=(count /...  25.1 us
    pallas_call x1, Pallas kernels, advantage(): pl.pallas_call(advantage_body, grid=(envs // LANES,), in_specs=[SMEM, col...  10.3 us
    pallas_call x2, Pallas kernels, normalized(): pl.pallas_call(functools.partial(normal_body, parts, len(states), float(c...  6.56 us
    pallas_call x1, Pallas kernels, summary(): pl.pallas_call(summary_body, grid=(groups,), in_specs=[SMEM, columns(SEG,...  6.39 us
    ppermute x4, waiting for transfers between devices, around(): lax.ppermute(state, axis, [(i, (i + far) % size) for i in range(size)])  5.08 us
    ppermute x4, starting transfers between devices, around(): lax.ppermute(state, axis, [(i, (i + far) % size) for i in range(size)])  4.53 us
  transfers between devices with their start and end apart: 9, of which 8 were waited for; matrix products, arithmetic and copies ran while one was open for 0% of the time, Pallas kernels for 26%

profile of v4, /device:TPU:0, one launch (start us, length us, event | category | flops | bytes accessed | tf_op | source)
XLA Modules:
  0.0 133.9 jit_solution(3052249462026359083)
XLA Ops:
  1.4 6.4 %conditional.2 = ((f32[3,32,512]{2,1,0:T(8,128)S(1)}, f32[16,128]{1,0:T(8,128)S(1)})) conditional(s32[]{:T(128)} %convert_element_type.4, () %tuple.27, (f32[2048,512]{1,0:T(8,128)}, f32[2048,512]{1,0:T(8,128)}, s32[3]{0:T(128)S(1)}, s32[4,512]{1,0:T(4,128)}, s32[1,512]{1,0:T(1,128)}, /*index=5*/f32[1,512]{1,0:T(1,128)S(1)}, ...), branch_computations={%region_0.0_spmd, %region_1.0_spmd} | conditional | flops 16777216 | bytes 8388616 | solution.py:428
  1.4 6.4 %summary.2 = (f32[3,32,512]{2,1,0:T(8,128)S(1)}, f32[16,128]{1,0:T(8,128)S(1)}) custom-call(s32[3]{0:T(128)S(1)} %get-tuple-element.32.here_ref, f32[32,64,512]{2,1,0:T(8,128)} %bitcast.18, f32[32,64,512]{2,1,0:T(8,128)} %bitcast.15, s32[4,512]{1,0:T(4,128)} %get-tuple-element.35.refs_0_, s32[1,512]{1,0:T(1,128)} %get-tuple-element.36.refs_1_, ...), custom_call_target="tpu_custom_call" | custom-call | flops 16777216 | bytes 8388608 | tf_op jit(solution)/shard_map/cond/branch_1_fun/summary/pallas_call | solution.py:158
  7.8 3.6 %pack.5 = f32[16,128,128]{2,1,0:T(8,128)} custom-call(f32[2048,512]{1,0:T(8,128)} %refs_0_.4), custom_call_target="tpu_custom_call" | custom-call | bytes 2097152 | tf_op jit(solution)/shard_map/pack/pallas_call | solution.py:64
  11.5 8.1 %all-to-all-start = ((f32[16,128,128]{2,1,0:T(8,128)}), f32[16,128,128]{2,1,0:T(8,128)S(1)}, u32[]{:S(2)}, u32[]{:S(2)}) async-start(f32[16,128,128]{2,1,0:T(8,128)} %pack.5), calls=%async_computation | async-start | bytes 2097152 | tf_op jit(solution)/shard_map/all_to_all | solution.py:404
  19.6 3.4 %pack.7 = f32[16,144,128]{2,1,0:T(8,128)} custom-call(f32[2048,512]{1,0:T(8,128)} %refs_0_.4, f32[16,128]{1,0:T(8,128)S(1)} %get-tuple-element.78.refs_1_), custom_call_target="tpu_custom_call" | custom-call | bytes 2097152 | tf_op jit(solution)/shard_map/pack/pallas_call | solution.py:64
  23.0 9.5 %all-to-all-done.refs_3_ = f32[16,128,128]{2,1,0:T(8,128)S(1)} async-done(((f32[16,128,128]{2,1,0:T(8,128)}), f32[16,128,128]{2,1,0:T(8,128)S(1)}, u32[]{:S(2)}, u32[]{:S(2)}) %all-to-all-start) | async-done | bytes 1048608 | tf_op jit(solution)/shard_map/all_to_all | solution.py:404
  32.5 3.7 %all-to-all-start.1 = ((f32[16,144,128]{2,1,0:T(8,128)}), f32[16,144,128]{2,1,0:T(8,128)S(1)}, u32[]{:S(2)}, u32[]{:S(2)}) async-start(f32[16,144,128]{2,1,0:T(8,128)} %pack.7), calls=%async_computation.1 | async-start | bytes 2359296 | tf_op jit(solution)/shard_map/all_to_all | solution.py:404
  36.2 6.1 %pack.6 = f32[16,256,128]{2,1,0:T(8,128)} custom-call(f32[2048,512]{1,0:T(8,128)} %refs_0_.4), custom_call_target="tpu_custom_call" | custom-call | bytes 4194304 | tf_op jit(solution)/shard_map/pack/pallas_call | solution.py:64
  42.3 7.6 %all-to-all-done.1.refs_4_ = f32[16,144,128]{2,1,0:T(8,128)S(1)} async-done(((f32[16,144,128]{2,1,0:T(8,128)}), f32[16,144,128]{2,1,0:T(8,128)S(1)}, u32[]{:S(2)}, u32[]{:S(2)}) %all-to-all-start.1) | async-done | bytes 1179680 | tf_op jit(solution)/shard_map/all_to_all | solution.py:404
  49.9 3.7 %all-to-all-start.2 = ((f32[16,256,128]{2,1,0:T(8,128)}), f32[16,256,128]{2,1,0:T(8,128)S(1)}, u32[]{:S(2)}, u32[]{:S(2)}) async-start(f32[16,256,128]{2,1,0:T(8,128)} %pack.6), calls=%async_computation.2 | async-start | bytes 4194304 | tf_op jit(solution)/shard_map/all_to_all | solution.py:404
  54.3 10.3 %advantage.1 = (f32[32,64,512]{2,1,0:T(8,128)}, f32[8,128]{1,0:T(8,128)}) custom-call(s32[3]{0:T(128)S(1)} %pad_add_fusion.here_ref, f32[32,64,512]{2,1,0:T(8,128)} %bitcast.17, f32[32,64,512]{2,1,0:T(8,128)} %bitcast.14, s32[4,512]{1,0:T(4,128)S(1)} %bitcast.24, s32[1,512]{1,0:T(1,128)S(1)} %bitcast.33, f32[1,512]{1,0:T(1,128)S(1)} %bitcast.30, ...), custom_call_target="tpu_custom_call" | custom-call | flops 25165824 | bytes 12582912 | tf_op jit(solution)/shard_map/advantage/pallas_call | solution.py:249
  64.6 5.9 %pack.9 = f32[16,264,128]{2,1,0:T(8,128)} custom-call(f32[2048,512]{1,0:T(8,128)} %bitcast.20, f32[8,128]{1,0:T(8,128)} %get-tuple-element.83.refs_1_), custom_call_target="tpu_custom_call" | custom-call | bytes 4194304 | tf_op jit(solution)/shard_map/pack/pallas_call | solution.py:64
  70.5 3.9 %all-to-all-done.2.refs_3_ = f32[16,256,128]{2,1,0:T(8,128)S(1)} async-done(((f32[16,256,128]{2,1,0:T(8,128)}), f32[16,256,128]{2,1,0:T(8,128)S(1)}, u32[]{:S(2)}, u32[]{:S(2)}) %all-to-all-start.2) | async-done | bytes 2097184 | tf_op jit(solution)/shard_map/all_to_all | solution.py:404
  74.4 1.3 copy-done
  75.7 6.2 %all-to-all-start.3 = ((f32[16,264,128]{2,1,0:T(8,128)}), f32[16,264,128]{2,1,0:T(8,128)S(1)}, u32[]{:S(2)}, u32[]{:S(2)}) async-start(f32[16,264,128]{2,1,0:T(8,128)} %pack.9), calls=%async_computation.3 | async-start | bytes 4325376 | tf_op jit(solution)/shard_map/all_to_all | solution.py:404
  81.9 6.1 %pack.8 = f32[16,256,128]{2,1,0:T(8,128)} custom-call(f32[2048,512]{1,0:T(8,128)} %bitcast.21), custom_call_target="tpu_custom_call" | custom-call | bytes 4194304 | tf_op jit(solution)/shard_map/pack/pallas_call | solution.py:64
  88.0 14.3 %all-to-all-done.3.part_ref.refs_2_ = f32[16,264,128]{2,1,0:T(8,128)S(1)} async-done(((f32[16,264,128]{2,1,0:T(8,128)}), f32[16,264,128]{2,1,0:T(8,128)S(1)}, u32[]{:S(2)}, u32[]{:S(2)}) %all-to-all-start.3) | async-done | bytes 2162720 | tf_op jit(solution)/shard_map/all_to_all | solution.py:404
  102.3 7.2 %all-to-all-start.4 = ((f32[16,256,128]{2,1,0:T(8,128)}), f32[16,256,128]{2,1,0:T(8,128)}, u32[]{:S(2)}, u32[]{:S(2)}) async-start(f32[16,256,128]{2,1,0:T(8,128)} %pack.8), calls=%async_computation.4 | async-start | bytes 4194304 | tf_op jit(solution)/shard_map/all_to_all | solution.py:404
  109.8 2.8 %collective-permute-start.2 = (f32[8,128]{1,0:T(8,128)S(1)}, f32[8,128]{1,0:T(8,128)S(1)}, u32[]{:S(2)}, u32[]{:S(2)}) collective-permute-start(f32[8,128]{1,0:T(8,128)S(1)} %gathered.1.refs_0_), channel_id=1, source_target_pairs={{0,6},{2,0},{4,2},{6,4},{1,7},{3,1},{5,3},{7,5},{8,14},{10,8},{12,... | collective-permute-start | bytes 12296 | tf_op jit(solution)/shard_map/ppermute | solution.py:330
  114.3 3.4 %collective-permute-done.1.refs_2_ = f32[8,128]{1,0:T(8,128)S(1)} collective-permute-done((f32[8,128]{1,0:T(8,128)S(1)}, f32[8,128]{1,0:T(8,128)S(1)}, u32[]{:S(2)}, u32[]{:S(2)}) %collective-permute-start.1) | collective-permute-done | bytes 4128 | tf_op jit(solution)/shard_map/ppermute | solution.py:330
  119.5 2.5 %normalized.2 = (f32[32,32768]{1,0:T(8,128)}, f32[32,32768]{1,0:T(8,128)}) custom-call(f32[8,128]{1,0:T(8,128)S(1)} %merge.1.refs_0_, f32[8,128]{1,0:T(8,128)S(1)} %collective-permute-done.3.refs_1_, f32[16,264,128]{2,1,0:T(8,128)S(1)} %all-to-all-done.3.part_ref.refs_2_, f32[16,128,128]{2,1,0:T(8,128)S(1)} %copy-done.3, ...), custom_call_target="tpu_custom_call" | custom-call | flops 2097152 | bytes 8388608 | tf_op jit(solution)/shard_map/normalized/pallas_call | solution.py:384
  122.0 6.2 %all-to-all-done.4.refs_2_ = f32[16,256,128]{2,1,0:T(8,128)} async-done(((f32[16,256,128]{2,1,0:T(8,128)}), f32[16,256,128]{2,1,0:T(8,128)}, u32[]{:S(2)}, u32[]{:S(2)}) %all-to-all-start.4) | async-done | bytes 2097184 | tf_op jit(solution)/shard_map/all_to_all | solution.py:404
  128.2 1.6 %copy-done.1 = f32[16,256,128]{2,1,0:T(8,128)S(1)} copy-done((f32[16,256,128]{2,1,0:T(8,128)S(1)}, f32[16,256,128]{2,1,0:T(8,128)}, u32[]{:S(2)}) %copy-start.1) | copy-done | bytes 2097176
  129.8 4.1 %normalized.3 = (f32[32,32768]{1,0:T(8,128)}, f32[32,32768]{1,0:T(8,128)}) custom-call(f32[8,128]{1,0:T(8,128)S(1)} %merge.1.refs_0_, f32[8,128]{1,0:T(8,128)S(1)} %collective-permute-done.3.refs_1_, f32[16,256,128]{2,1,0:T(8,128)} %all-to-all-done.4.refs_2_, f32[16,256,128]{2,1,0:T(8,128)S(1)} %copy-done.1, ...), custom_call_target="tpu_custom_call", output_to_operand_aliasing={{0}: (4, {}), {1}: (5, {})} | custom-call | flops 2097152 | bytes 8388608 | tf_op jit(solution)/shard_map/normalized/pallas_call | solution.py:384
  (22 shorter events, 5.2 us)
Async XLA Ops:
  7.8 3.6 %copy-start.4 = (s32[512,4]{0,1:T(4,128)S(1)}, s32[512,4]{0,1:T(4,128)}, u32[]{:S(2)}) copy-start(s32[512,4]{0,1:T(4,128)} %param.14) | copy-start | bytes 24580
  7.8 3.6 %copy-start.5 = (s32[512]{0:T(512)S(1)}, s32[512]{0:T(512)}, u32[]{:S(2)}) copy-start(s32[512]{0:T(512)} %param.15) | copy-start | bytes 6148
  11.5 21.0 %all-to-all-start = ((f32[16,128,128]{2,1,0:T(8,128)}), f32[16,128,128]{2,1,0:T(8,128)S(1)}, u32[]{:S(2)}, u32[]{:S(2)}) async-start(f32[16,128,128]{2,1,0:T(8,128)} %pack.5), calls=%async_computation | async-start | bytes 2097152 | tf_op jit(solution)/shard_map/all_to_all | solution.py:404
  32.5 9.8 %copy-start.2 = (f32[16,128,128]{2,1,0:T(8,128)}, f32[16,128,128]{2,1,0:T(8,128)S(1)}, u32[]{:S(2)}) copy-start(f32[16,128,128]{2,1,0:T(8,128)S(1)} %all-to-all-done.refs_3_) | copy-start | bytes 3145732
  32.5 17.4 %all-to-all-start.1 = ((f32[16,144,128]{2,1,0:T(8,128)}), f32[16,144,128]{2,1,0:T(8,128)S(1)}, u32[]{:S(2)}, u32[]{:S(2)}) async-start(f32[16,144,128]{2,1,0:T(8,128)} %pack.7), calls=%async_computation.1 | async-start | bytes 2359296 | tf_op jit(solution)/shard_map/all_to_all | solution.py:404
  49.9 24.5 %all-to-all-start.2 = ((f32[16,256,128]{2,1,0:T(8,128)}), f32[16,256,128]{2,1,0:T(8,128)S(1)}, u32[]{:S(2)}, u32[]{:S(2)}) async-start(f32[16,256,128]{2,1,0:T(8,128)} %pack.6), calls=%async_computation.2 | async-start | bytes 4194304 | tf_op jit(solution)/shard_map/all_to_all | solution.py:404
  74.4 1.3 copy-start
  75.7 26.6 %all-to-all-start.3 = ((f32[16,264,128]{2,1,0:T(8,128)}), f32[16,264,128]{2,1,0:T(8,128)S(1)}, u32[]{:S(2)}, u32[]{:S(2)}) async-start(f32[16,264,128]{2,1,0:T(8,128)} %pack.9), calls=%async_computation.3 | async-start | bytes 4325376 | tf_op jit(solution)/shard_map/all_to_all | solution.py:404
  102.3 25.8 %all-to-all-start.4 = ((f32[16,256,128]{2,1,0:T(8,128)}), f32[16,256,128]{2,1,0:T(8,128)}, u32[]{:S(2)}, u32[]{:S(2)}) async-start(f32[16,256,128]{2,1,0:T(8,128)} %pack.8), calls=%async_computation.4 | async-start | bytes 4194304 | tf_op jit(solution)/shard_map/all_to_all | solution.py:404
  109.5 10.0 %copy-start.3 = (f32[16,128,128]{2,1,0:T(8,128)S(1)}, f32[16,128,128]{2,1,0:T(8,128)}, u32[]{:S(2)}) copy-start(f32[16,128,128]{2,1,0:T(8,128)} %copy-done.2) | copy-start | bytes 3145732
  109.8 4.5 %collective-permute-start.2 = (f32[8,128]{1,0:T(8,128)S(1)}, f32[8,128]{1,0:T(8,128)S(1)}, u32[]{:S(2)}, u32[]{:S(2)}) collective-permute-start(f32[8,128]{1,0:T(8,128)S(1)} %gathered.1.refs_0_), channel_id=1, source_target_pairs={{0,6},{2,0},{4,2},{6,4},{1,7},{3,1},{5,3},{7,5},{8,14},{10,8},{12,... | collective-permute-start | bytes 12296 | tf_op jit(solution)/shard_map/ppermute | solution.py:330
  112.6 5.1 %collective-permute-start.1 = (f32[8,128]{1,0:T(8,128)S(1)}, f32[8,128]{1,0:T(8,128)S(1)}, u32[]{:S(2)}, u32[]{:S(2)}) collective-permute-start(f32[8,128]{1,0:T(8,128)S(1)} %gathered.1.refs_0_), channel_id=1, source_target_pairs={{0,4},{2,6},{4,0},{6,2},{1,5},{3,7},{5,1},{7,3},{8,12},{10,14},{12... | collective-permute-start | bytes 12296 | tf_op jit(solution)/shard_map/ppermute | solution.py:330
  113.4 4.8 %collective-permute-start = (f32[8,128]{1,0:T(8,128)S(1)}, f32[8,128]{1,0:T(8,128)S(1)}, u32[]{:S(2)}, u32[]{:S(2)}) collective-permute-start(f32[8,128]{1,0:T(8,128)S(1)} %gathered.1.refs_0_), channel_id=1, source_target_pairs={{0,2},{2,4},{4,6},{6,0},{1,3},{3,5},{5,7},{7,1},{8,10},{10,12},{12... | collective-permute-start | bytes 12296 | tf_op jit(solution)/shard_map/ppermute | solution.py:330
  118.3 1.2 collective-permute-start.3
  128.2 1.6 %copy-start.1 = (f32[16,256,128]{2,1,0:T(8,128)S(1)}, f32[16,256,128]{2,1,0:T(8,128)}, u32[]{:S(2)}) copy-start(f32[16,256,128]{2,1,0:T(8,128)} %copy-done) | copy-start | bytes 6291460

commit v5 on v4

--- a/solution.py
+++ b/solution.py
@@ -15,7 +15,7 @@
 F32 = jnp.float32
 LANES = 128
 SEG = 32
-ROWS = 128
+ROWS = 512
 SMEM = pl.BlockSpec(memory_space=pltpu.SMEM)
 ANY = pl.BlockSpec(memory_space=pl.ANY)
 VMEM = pl.BlockSpec(memory_space=pltpu.VMEM)

time: 135 us -> 131 us (0.970)
  Pallas kernels: 48.7 us -> 37.8 us
  waiting for transfers between devices: 46.6 us -> 54.6 us
    pallas_call x5, Pallas kernels: 25.1 us -> 14.2 us  [pack(): pl.pallas_call(functools.partial(pack_body, dests, riders), grid=(count /...]
    all_to_all x5, waiting for transfers between devices: 41.5 us -> 49.5 us  [exchange(): return (lax.all_to_all(packed, TM, 0, 0, tiled=True), behind)]
  transfers between devices with their start and end apart: 9 -> 9, of which waited for: 8 -> 8; matrix products, arithmetic and copies ran while one was open for 0% -> 1% of each run, Pallas kernels for 26% -> 19%
where the time goes in v5:
time: 131 us; the launch traced here: 130 us
  waiting for transfers between devices  54.6 us (42%)
  Pallas kernels  37.8 us (29%)
  starting transfers between devices  32.3 us (25%)
  local copies, waits for them, and re-layouts  3.61 us (3%)
    all_to_all x5, waiting for transfers between devices, exchange(): return (lax.all_to_all(packed, TM, 0, 0, tiled=True), behind)  49.5 us
    all_to_all x5, starting transfers between devices, exchange(): return (lax.all_to_all(packed, TM, 0, 0, tiled=True), behind)  27.8 us
    pallas_call x5, Pallas kernels, pack(): pl.pallas_call(functools.partial(pack_body, dests, riders), grid=(count /...  14.2 us
    pallas_call x1, Pallas kernels, advantage(): pl.pallas_call(advantage_body, grid=(envs // LANES,), in_specs=[SMEM, col...  10.3 us
    pallas_call x2, Pallas kernels, normalized(): pl.pallas_call(functools.partial(normal_body, parts, len(states), float(c...  6.56 us
    pallas_call x1, Pallas kernels, summary(): pl.pallas_call(summary_body, grid=(groups,), in_specs=[SMEM, columns(SEG,...  6.39 us
    ppermute x4, waiting for transfers between devices, around(): lax.ppermute(state, axis, [(i, (i + far) % size) for i in range(size)])  5.08 us
    ppermute x4, starting transfers between devices, around(): lax.ppermute(state, axis, [(i, (i + far) % size) for i in range(size)])  4.53 us
  transfers between devices with their start and end apart: 9, of which 8 were waited for; matrix products, arithmetic and copies ran while one was open for 1% of the time, Pallas kernels for 19%

profile of v5, /device:TPU:0, one launch (start us, length us, event | category | flops | bytes accessed | tf_op | source)
XLA Modules:
  0.0 129.9 jit_solution(8425388650776778146)
XLA Ops:
  1.4 6.4 %conditional.2 = ((f32[3,32,512]{2,1,0:T(8,128)S(1)}, f32[16,128]{1,0:T(8,128)S(1)})) conditional(s32[]{:T(128)} %convert_element_type.4, () %tuple.27, (f32[2048,512]{1,0:T(8,128)}, f32[2048,512]{1,0:T(8,128)}, s32[3]{0:T(128)S(1)}, s32[4,512]{1,0:T(4,128)}, s32[1,512]{1,0:T(1,128)}, /*index=5*/f32[1,512]{1,0:T(1,128)S(1)}, ...), branch_computations={%region_0.0_spmd, %region_1.0_spmd} | conditional | flops 16777216 | bytes 8388616 | solution.py:428
  1.4 6.4 %summary.2 = (f32[3,32,512]{2,1,0:T(8,128)S(1)}, f32[16,128]{1,0:T(8,128)S(1)}) custom-call(s32[3]{0:T(128)S(1)} %get-tuple-element.32.here_ref, f32[32,64,512]{2,1,0:T(8,128)} %bitcast.18, f32[32,64,512]{2,1,0:T(8,128)} %bitcast.15, s32[4,512]{1,0:T(4,128)} %get-tuple-element.35.refs_0_, s32[1,512]{1,0:T(1,128)} %get-tuple-element.36.refs_1_, ...), custom_call_target="tpu_custom_call" | custom-call | flops 16777216 | bytes 8388608 | tf_op jit(solution)/shard_map/cond/branch_1_fun/summary/pallas_call | solution.py:158
  7.8 2.5 %pack.5 = f32[16,128,128]{2,1,0:T(8,128)} custom-call(f32[2048,512]{1,0:T(8,128)} %refs_0_.4), custom_call_target="tpu_custom_call" | custom-call | bytes 2097152 | tf_op jit(solution)/shard_map/pack/pallas_call | solution.py:64
  10.4 8.1 %all-to-all-start = ((f32[16,128,128]{2,1,0:T(8,128)}), f32[16,128,128]{2,1,0:T(8,128)S(1)}, u32[]{:S(2)}, u32[]{:S(2)}) async-start(f32[16,128,128]{2,1,0:T(8,128)} %pack.5), calls=%async_computation | async-start | bytes 2097152 | tf_op jit(solution)/shard_map/all_to_all | solution.py:404
  18.6 2.6 %pack.7 = f32[16,144,128]{2,1,0:T(8,128)} custom-call(f32[2048,512]{1,0:T(8,128)} %refs_0_.4, f32[16,128]{1,0:T(8,128)S(1)} %get-tuple-element.78.refs_1_), custom_call_target="tpu_custom_call" | custom-call | bytes 2097152 | tf_op jit(solution)/shard_map/pack/pallas_call | solution.py:64
  21.1 10.3 %all-to-all-done.refs_3_ = f32[16,128,128]{2,1,0:T(8,128)S(1)} async-done(((f32[16,128,128]{2,1,0:T(8,128)}), f32[16,128,128]{2,1,0:T(8,128)S(1)}, u32[]{:S(2)}, u32[]{:S(2)}) %all-to-all-start) | async-done | bytes 1048608 | tf_op jit(solution)/shard_map/all_to_all | solution.py:404
  31.5 3.7 %all-to-all-start.1 = ((f32[16,144,128]{2,1,0:T(8,128)}), f32[16,144,128]{2,1,0:T(8,128)S(1)}, u32[]{:S(2)}, u32[]{:S(2)}) async-start(f32[16,144,128]{2,1,0:T(8,128)} %pack.7), calls=%async_computation.1 | async-start | bytes 2359296 | tf_op jit(solution)/shard_map/all_to_all | solution.py:404
  35.2 2.9 %pack.6 = f32[16,256,128]{2,1,0:T(8,128)} custom-call(f32[2048,512]{1,0:T(8,128)} %refs_0_.4), custom_call_target="tpu_custom_call" | custom-call | bytes 4194304 | tf_op jit(solution)/shard_map/pack/pallas_call | solution.py:64
  38.1 10.8 %all-to-all-done.1.refs_4_ = f32[16,144,128]{2,1,0:T(8,128)S(1)} async-done(((f32[16,144,128]{2,1,0:T(8,128)}), f32[16,144,128]{2,1,0:T(8,128)S(1)}, u32[]{:S(2)}, u32[]{:S(2)}) %all-to-all-start.1) | async-done | bytes 1179680 | tf_op jit(solution)/shard_map/all_to_all | solution.py:404
  48.9 3.7 %all-to-all-start.2 = ((f32[16,256,128]{2,1,0:T(8,128)}), f32[16,256,128]{2,1,0:T(8,128)S(1)}, u32[]{:S(2)}, u32[]{:S(2)}) async-start(f32[16,256,128]{2,1,0:T(8,128)} %pack.6), calls=%async_computation.2 | async-start | bytes 4194304 | tf_op jit(solution)/shard_map/all_to_all | solution.py:404
  53.3 10.3 %advantage.1 = (f32[32,64,512]{2,1,0:T(8,128)}, f32[8,128]{1,0:T(8,128)}) custom-call(s32[3]{0:T(128)S(1)} %pad_add_fusion.here_ref, f32[32,64,512]{2,1,0:T(8,128)} %bitcast.17, f32[32,64,512]{2,1,0:T(8,128)} %bitcast.14, s32[4,512]{1,0:T(4,128)S(1)} %bitcast.24, s32[1,512]{1,0:T(1,128)S(1)} %bitcast.33, f32[1,512]{1,0:T(1,128)S(1)} %bitcast.30, ...), custom_call_target="tpu_custom_call" | custom-call | flops 25165824 | bytes 12582912 | tf_op jit(solution)/shard_map/advantage/pallas_call | solution.py:249
  63.6 3.3 %pack.9 = f32[16,264,128]{2,1,0:T(8,128)} custom-call(f32[2048,512]{1,0:T(8,128)} %bitcast.20, f32[8,128]{1,0:T(8,128)} %get-tuple-element.83.refs_1_), custom_call_target="tpu_custom_call" | custom-call | bytes 4194304 | tf_op jit(solution)/shard_map/pack/pallas_call | solution.py:64
  66.8 5.6 %all-to-all-done.2.refs_3_ = f32[16,256,128]{2,1,0:T(8,128)S(1)} async-done(((f32[16,256,128]{2,1,0:T(8,128)}), f32[16,256,128]{2,1,0:T(8,128)S(1)}, u32[]{:S(2)}, u32[]{:S(2)}) %all-to-all-start.2) | async-done | bytes 2097184 | tf_op jit(solution)/shard_map/all_to_all | solution.py:404
  72.4 1.3 %copy-done = f32[16,256,128]{2,1,0:T(8,128)} copy-done((f32[16,256,128]{2,1,0:T(8,128)}, f32[16,256,128]{2,1,0:T(8,128)S(1)}, u32[]{:S(2)}) %copy-start) | copy-done | bytes 2097176
  73.7 5.9 %all-to-all-start.3 = ((f32[16,264,128]{2,1,0:T(8,128)}), f32[16,264,128]{2,1,0:T(8,128)S(1)}, u32[]{:S(2)}, u32[]{:S(2)}) async-start(f32[16,264,128]{2,1,0:T(8,128)} %pack.9), calls=%async_computation.3 | async-start | bytes 4325376 | tf_op jit(solution)/shard_map/all_to_all | solution.py:404
  79.7 2.9 %pack.8 = f32[16,256,128]{2,1,0:T(8,128)} custom-call(f32[2048,512]{1,0:T(8,128)} %bitcast.21), custom_call_target="tpu_custom_call" | custom-call | bytes 4194304 | tf_op jit(solution)/shard_map/pack/pallas_call | solution.py:64
  82.6 16.7 %all-to-all-done.3.part_ref.refs_2_ = f32[16,264,128]{2,1,0:T(8,128)S(1)} async-done(((f32[16,264,128]{2,1,0:T(8,128)}), f32[16,264,128]{2,1,0:T(8,128)S(1)}, u32[]{:S(2)}, u32[]{:S(2)}) %all-to-all-start.3) | async-done | bytes 2162720 | tf_op jit(solution)/shard_map/all_to_all | solution.py:404
  99.3 6.3 %all-to-all-start.4 = ((f32[16,256,128]{2,1,0:T(8,128)}), f32[16,256,128]{2,1,0:T(8,128)}, u32[]{:S(2)}, u32[]{:S(2)}) async-start(f32[16,256,128]{2,1,0:T(8,128)} %pack.8), calls=%async_computation.4 | async-start | bytes 4194304 | tf_op jit(solution)/shard_map/all_to_all | solution.py:404
  105.9 2.8 %collective-permute-start.2 = (f32[8,128]{1,0:T(8,128)S(1)}, f32[8,128]{1,0:T(8,128)S(1)}, u32[]{:S(2)}, u32[]{:S(2)}) collective-permute-start(f32[8,128]{1,0:T(8,128)S(1)} %gathered.1.refs_0_), channel_id=1, source_target_pairs={{0,6},{2,0},{4,2},{6,4},{1,7},{3,1},{5,3},{7,5},{8,14},{10,8},{12,... | collective-permute-start | bytes 12296 | tf_op jit(solution)/shard_map/ppermute | solution.py:330
  110.4 3.4 %collective-permute-done.1.refs_2_ = f32[8,128]{1,0:T(8,128)S(1)} collective-permute-done((f32[8,128]{1,0:T(8,128)S(1)}, f32[8,128]{1,0:T(8,128)S(1)}, u32[]{:S(2)}, u32[]{:S(2)}) %collective-permute-start.1) | collective-permute-done | bytes 4128 | tf_op jit(solution)/shard_map/ppermute | solution.py:330
  115.6 2.5 %normalized.2 = (f32[32,32768]{1,0:T(8,128)}, f32[32,32768]{1,0:T(8,128)}) custom-call(f32[8,128]{1,0:T(8,128)S(1)} %merge.1.refs_0_, f32[8,128]{1,0:T(8,128)S(1)} %collective-permute-done.3.refs_1_, f32[16,264,128]{2,1,0:T(8,128)S(1)} %all-to-all-done.3.part_ref.refs_2_, f32[16,128,128]{2,1,0:T(8,128)S(1)} %copy-done.3, ...), custom_call_target="tpu_custom_call" | custom-call | flops 2097152 | bytes 8388608 | tf_op jit(solution)/shard_map/normalized/pallas_call | solution.py:384
  118.1 6.1 %all-to-all-done.4.refs_2_ = f32[16,256,128]{2,1,0:T(8,128)} async-done(((f32[16,256,128]{2,1,0:T(8,128)}), f32[16,256,128]{2,1,0:T(8,128)}, u32[]{:S(2)}, u32[]{:S(2)}) %all-to-all-start.4) | async-done | bytes 2097184 | tf_op jit(solution)/shard_map/all_to_all | solution.py:404
  124.2 1.6 %copy-done.1 = f32[16,256,128]{2,1,0:T(8,128)S(1)} copy-done((f32[16,256,128]{2,1,0:T(8,128)S(1)}, f32[16,256,128]{2,1,0:T(8,128)}, u32[]{:S(2)}) %copy-start.1) | copy-done | bytes 2097176
  125.8 4.1 %normalized.3 = (f32[32,32768]{1,0:T(8,128)}, f32[32,32768]{1,0:T(8,128)}) custom-call(f32[8,128]{1,0:T(8,128)S(1)} %merge.1.refs_0_, f32[8,128]{1,0:T(8,128)S(1)} %collective-permute-done.3.refs_1_, f32[16,256,128]{2,1,0:T(8,128)} %all-to-all-done.4.refs_2_, f32[16,256,128]{2,1,0:T(8,128)S(1)} %copy-done.1, ...), custom_call_target="tpu_custom_call", output_to_operand_aliasing={{0}: (4, {}), {1}: (5, {})} | custom-call | flops 2097152 | bytes 8388608 | tf_op jit(solution)/shard_map/normalized/pallas_call | solution.py:384
  (22 shorter events, 5.2 us)
Async XLA Ops:
  7.8 2.6 %copy-start.4 = (s32[512,4]{0,1:T(4,128)S(1)}, s32[512,4]{0,1:T(4,128)}, u32[]{:S(2)}) copy-start(s32[512,4]{0,1:T(4,128)} %param.14) | copy-start | bytes 24580
  7.8 2.6 %copy-start.5 = (s32[512]{0:T(512)S(1)}, s32[512]{0:T(512)}, u32[]{:S(2)}) copy-start(s32[512]{0:T(512)} %param.15) | copy-start | bytes 6148
  10.4 21.1 %all-to-all-start = ((f32[16,128,128]{2,1,0:T(8,128)}), f32[16,128,128]{2,1,0:T(8,128)S(1)}, u32[]{:S(2)}, u32[]{:S(2)}) async-start(f32[16,128,128]{2,1,0:T(8,128)} %pack.5), calls=%async_computation | async-start | bytes 2097152 | tf_op jit(solution)/shard_map/all_to_all | solution.py:404
  31.5 6.6 %copy-start.2 = (f32[16,128,128]{2,1,0:T(8,128)}, f32[16,128,128]{2,1,0:T(8,128)S(1)}, u32[]{:S(2)}) copy-start(f32[16,128,128]{2,1,0:T(8,128)S(1)} %all-to-all-done.refs_3_) | copy-start | bytes 3145732
  31.5 17.4 %all-to-all-start.1 = ((f32[16,144,128]{2,1,0:T(8,128)}), f32[16,144,128]{2,1,0:T(8,128)S(1)}, u32[]{:S(2)}, u32[]{:S(2)}) async-start(f32[16,144,128]{2,1,0:T(8,128)} %pack.7), calls=%async_computation.1 | async-start | bytes 2359296 | tf_op jit(solution)/shard_map/all_to_all | solution.py:404
  48.9 23.5 %all-to-all-start.2 = ((f32[16,256,128]{2,1,0:T(8,128)}), f32[16,256,128]{2,1,0:T(8,128)S(1)}, u32[]{:S(2)}, u32[]{:S(2)}) async-start(f32[16,256,128]{2,1,0:T(8,128)} %pack.6), calls=%async_computation.2 | async-start | bytes 4194304 | tf_op jit(solution)/shard_map/all_to_all | solution.py:404
  72.4 1.3 %copy-start = (f32[16,256,128]{2,1,0:T(8,128)}, f32[16,256,128]{2,1,0:T(8,128)S(1)}, u32[]{:S(2)}) copy-start(f32[16,256,128]{2,1,0:T(8,128)S(1)} %all-to-all-done.2.refs_3_) | copy-start | bytes 6291460
  73.7 25.5 %all-to-all-start.3 = ((f32[16,264,128]{2,1,0:T(8,128)}), f32[16,264,128]{2,1,0:T(8,128)S(1)}, u32[]{:S(2)}, u32[]{:S(2)}) async-start(f32[16,264,128]{2,1,0:T(8,128)} %pack.9), calls=%async_computation.3 | async-start | bytes 4325376 | tf_op jit(solution)/shard_map/all_to_all | solution.py:404
  99.3 25.0 %all-to-all-start.4 = ((f32[16,256,128]{2,1,0:T(8,128)}), f32[16,256,128]{2,1,0:T(8,128)}, u32[]{:S(2)}, u32[]{:S(2)}) async-start(f32[16,256,128]{2,1,0:T(8,128)} %pack.8), calls=%async_computation.4 | async-start | bytes 4194304 | tf_op jit(solution)/shard_map/all_to_all | solution.py:404
  105.6 10.0 %copy-start.3 = (f32[16,128,128]{2,1,0:T(8,128)S(1)}, f32[16,128,128]{2,1,0:T(8,128)}, u32[]{:S(2)}) copy-start(f32[16,128,128]{2,1,0:T(8,128)} %copy-done.2) | copy-start | bytes 3145732
  105.9 4.5 %collective-permute-start.2 = (f32[8,128]{1,0:T(8,128)S(1)}, f32[8,128]{1,0:T(8,128)S(1)}, u32[]{:S(2)}, u32[]{:S(2)}) collective-permute-start(f32[8,128]{1,0:T(8,128)S(1)} %gathered.1.refs_0_), channel_id=1, source_target_pairs={{0,6},{2,0},{4,2},{6,4},{1,7},{3,1},{5,3},{7,5},{8,14},{10,8},{12,... | collective-permute-start | bytes 12296 | tf_op jit(solution)/shard_map/ppermute | solution.py:330
  108.7 5.1 %collective-permute-start.1 = (f32[8,128]{1,0:T(8,128)S(1)}, f32[8,128]{1,0:T(8,128)S(1)}, u32[]{:S(2)}, u32[]{:S(2)}) collective-permute-start(f32[8,128]{1,0:T(8,128)S(1)} %gathered.1.refs_0_), channel_id=1, source_target_pairs={{0,4},{2,6},{4,0},{6,2},{1,5},{3,7},{5,1},{7,3},{8,12},{10,14},{12... | collective-permute-start | bytes 12296 | tf_op jit(solution)/shard_map/ppermute | solution.py:330
  109.5 4.8 %collective-permute-start = (f32[8,128]{1,0:T(8,128)S(1)}, f32[8,128]{1,0:T(8,128)S(1)}, u32[]{:S(2)}, u32[]{:S(2)}) collective-permute-start(f32[8,128]{1,0:T(8,128)S(1)} %gathered.1.refs_0_), channel_id=1, source_target_pairs={{0,2},{2,4},{4,6},{6,0},{1,3},{3,5},{5,7},{7,1},{8,10},{10,12},{12... | collective-permute-start | bytes 12296 | tf_op jit(solution)/shard_map/ppermute | solution.py:330
  114.4 1.2 collective-permute-start.3
  124.2 1.6 %copy-start.1 = (f32[16,256,128]{2,1,0:T(8,128)S(1)}, f32[16,256,128]{2,1,0:T(8,128)}, u32[]{:S(2)}) copy-start(f32[16,256,128]{2,1,0:T(8,128)} %copy-done) | copy-start | bytes 6291460
